TPU v7x, 512 devices: a whole 4x4x16 slice. The times are simulated.
512 devices in a mesh: lat: 16 (over y, x), lon: 32 (over z, core).
Axes of the slice: x: 4, y: 4, z: 16, core: 2. Of those that a mesh axis runs over, the one named last changes fastest.
Arguments:
- prior_state: bfloat16 [2, 4, 80, 128, 4096], P(None, None, None, 'lat', 'lon'), may hold values from -6 to 6
- courant: float32 [2, 4, 128, 4096], P(None, None, 'lat', 'lon'), may hold values from -0.45 to 0.45
- obs_tile: int32 [64], replicated, may hold values from 0 to 511, as said below
- obs_site: int32 [64], replicated, may hold values from 0 to 8191
- obs_value: float32 [64], replicated, may hold values from -6 to 6
- obs_var: float32 [64], replicated, may hold values from 0.2 to 2
- loc_bits: int32 [64, 18], replicated, may hold values from 0 to 1073741823
- batch_order: int32 [4], replicated, may hold values from 0 to 3, each once
Outputs:
- analysis: bfloat16 [2, 4, 80, 128, 4096], P(None, None, None, 'lat', 'lon')
Inputs may be any that keep to these rules, and one draw needn't show every extreme that they name: `obs_tile`: in each batch of 16 consecutive observations one tile owns exactly 4 observations and every other tile at most one. `loc_bits`: bits of tiles numbered 512 or more are not read.
All inputs are finite; a program needn't handle non-finite values.
Results may differ from a plain program's by a relative error of at most 0.0013.
Values may be sent and summed in bfloat16 or wider, within the bound.
A program may use at most 64 MiB of HBM per device.

v0:
```python
import jax
import jax.numpy as jnp
from jax import lax
from jax.sharding import PartitionSpec as P

OBSERVED_BATCH = 16
BATCHES = 4
CAP = 4


EPSILON = 1e-05
HIGHEST_PRECISE = lax.Precision.HIGHEST


def padded(cells, sides, width, closed):
    for axis, dim in sides:
        count = lax.axis_size(axis)
        ends = count if closed else count - 1
        head = lax.slice_in_dim(cells, 0, width, axis=dim)
        tail = lax.slice_in_dim(cells, cells.shape[dim] - width, cells.shape[dim], axis=dim)
        cells = jnp.concatenate(
            [
                lax.ppermute(tail, axis, [(i, (i + 1) % count) for i in range(ends)]),
                cells,
                lax.ppermute(head, axis, [((i + 1) % count, i) for i in range(ends)]),
            ],
            axis=dim,
        )
    return cells


def upwind_transport(center_value, west, east, south, north, along_lon, along_lat):
    return (
        center_value
        - jnp.maximum(along_lon, 0.0) * (center_value - west)
        - jnp.minimum(along_lon, 0.0) * (east - center_value)
        - jnp.maximum(along_lat, 0.0) * (center_value - south)
        - jnp.minimum(along_lat, 0.0) * (north - center_value)
    )


def tile_bits(loc_bits, tile_ids):
    bit_words = jnp.take(loc_bits, tile_ids // 30, axis=1)
    return jnp.bitwise_and(jnp.right_shift(bit_words, (tile_ids % 30)[None, :]), 1).astype(
        jnp.float32
    )


def eakf_step(prior_row, obs_val, obs_err, member_list):
    mean_prior = jnp.mean(prior_row)
    anomaly = prior_row - mean_prior
    spread = jnp.sum(anomaly * anomaly) / (member_list - 1) + EPSILON
    post_var = spread * obs_err / (spread + obs_err)
    post_mean = post_var * (mean_prior / spread + obs_val / obs_err)
    factor = jnp.sqrt(obs_err / (spread + obs_err))
    increment = factor * anomaly + post_mean - prior_row
    weights = anomaly / ((member_list - 1) * spread)
    return (increment, weights)


def per_device(prior_state, courant, obs_tile, obs_site, obs_value, obs_var, loc_bits, batch_order):
    field_stack, level_list, member_list, rows_dev, cols_dev = prior_state.shape
    count_of_cells = rows_dev * cols_dev
    south_north = padded(prior_state, (("lat", 3),), 1, False)
    west_east = padded(prior_state, (("lon", 4),), 1, True)
    prediction = upwind_transport(
        prior_state.astype(jnp.float32),
        west_east[..., :-2].astype(jnp.float32),
        west_east[..., 2:].astype(jnp.float32),
        south_north[..., :-2, :].astype(jnp.float32),
        south_north[..., 2:, :].astype(jnp.float32),
        courant[0][None, :, None],
        courant[1][None, :, None],
    )
    flattened_prediction = prediction.reshape(field_stack * level_list, member_list, count_of_cells)
    tile_self = lax.axis_index("lat") * lax.axis_size("lon") + lax.axis_index("lon")
    own_bits = tile_bits(loc_bits, tile_self[None])[:, 0]
    identity = jnp.eye(member_list, dtype=jnp.float32)
    current_state = flattened_prediction
    lower_pair = lax.broadcasted_iota(
        jnp.int32, (OBSERVED_BATCH, OBSERVED_BATCH), 0
    ) < lax.broadcasted_iota(jnp.int32, (OBSERVED_BATCH, OBSERVED_BATCH), 1)
    for order_index in range(BATCHES):
        batch_offset = batch_order[order_index] * OBSERVED_BATCH
        owner_tiles = lax.dynamic_slice_in_dim(obs_tile, batch_offset, OBSERVED_BATCH)
        sites = lax.dynamic_slice_in_dim(obs_site, batch_offset, OBSERVED_BATCH)
        obs_values = lax.dynamic_slice_in_dim(obs_value, batch_offset, OBSERVED_BATCH)
        obs_errors = lax.dynamic_slice_in_dim(obs_var, batch_offset, OBSERVED_BATCH)
        batch_bits = lax.dynamic_slice_in_dim(loc_bits, batch_offset, OBSERVED_BATCH, 0)
        mine_mask = lax.dynamic_slice_in_dim(own_bits, batch_offset, OBSERVED_BATCH)
        plane_index = sites // count_of_cells
        cell_index = sites % count_of_cells
        owned_here = owner_tiles == tile_self
        local_prior = current_state[plane_index, :, cell_index]
        same_owner = owner_tiles[:, None] == owner_tiles[None, :]
        slot_rank = jnp.sum((same_owner & lower_pair).astype(jnp.int32), axis=0)
        slot_ids = jnp.arange(CAP, dtype=jnp.int32)
        selector = (owned_here[None, :] & (slot_rank[None, :] == slot_ids[:, None])).astype(
            jnp.float32
        )
        outgoing = jnp.dot(selector, local_prior, precision=HIGHEST_PRECISE)
        collected = lax.all_gather(outgoing, ("lat", "lon"), axis=0, tiled=True)
        prior_values = collected[owner_tiles * CAP + slot_rank]
        cross_mask = tile_bits(batch_bits, owner_tiles)

        def advance(obs_index, loop_state):
            prior_values, transform_now = loop_state
            increment, weights = eakf_step(
                prior_values[obs_index], obs_values[obs_index], obs_errors[obs_index], member_list
            )
            projected = jnp.dot(prior_values, weights, precision=HIGHEST_PRECISE)
            prior_values = (
                prior_values
                + cross_mask[obs_index][:, None] * projected[:, None] * increment[None, :]
            )
            turned = jnp.dot(transform_now, weights, precision=HIGHEST_PRECISE)
            transform_now = (
                transform_now + mine_mask[obs_index] * turned[:, None] * increment[None, :]
            )
            return (prior_values, transform_now)

        prior_values, transform_now = lax.fori_loop(
            0, OBSERVED_BATCH, advance, (prior_values, identity)
        )
        current_state = jnp.einsum(
            "pec,eg->pgc", current_state, transform_now, precision=HIGHEST_PRECISE
        )
    return current_state.reshape(field_stack, level_list, member_list, rows_dev, cols_dev).astype(
        jnp.bfloat16
    )


def solution(mesh):
    placed = (
        P(None, None, None, "lat", "lon"),
        P(None, None, "lat", "lon"),
        P(),
        P(),
        P(),
        P(),
        P(),
        P(),
    )
    return jax.shard_map(
        per_device,
        mesh=mesh,
        in_specs=placed,
        out_specs=P(None, None, None, "lat", "lon"),
        check_vma=False,
    )
```

profile of v0, /device:TPU:1, one launch (start us, length us, event | category | flops | bytes accessed | tf_op | source)
XLA Modules:
  0.0 1212.6 jit_solution(8700980762331117998)
XLA Ops:
  0.0 3.3 fusion.91
  3.4 2.3 copy.73
  5.6 3.0 collective-permute-start
  9.4 3.8 collective-permute-start.1
  13.7 1.3 collective-permute-start.2
  15.1 1.3 collective-permute-start.3
  27.9 1.7 copy.46
  30.2 5.6 fusion.23
  35.8 4.9 copy.51
  40.7 1.3 gather_fusion
  42.1 141.5 %all-gather = f32[512,4,80]{2,1,0:T(4,128)S(1)} all-gather(f32[1,4,80]{2,1,0:T(4,128)S(1)} %convolution_bitcast_fusion.14), channel_id=1, replica_groups=mesh['lat'=16,'lon'=32] {'lat','lon'}, dimensions={0}, use_global_device_ids=true | all-gather | bytes 656640 | tf_op jit(solution)/shard_map/all_gather | solution.py:102
  184.2 139.3 %while.61 = (s32[]{:T(128)}, f32[16,80]{1,0:T(8,128)S(1)}, f32[80,80]{1,0:T(8,128)S(1)}, f32[16,16]{1,0:T(8,128)S(1)}, f32[16]{0:T(128)S(1)}, /*index=5*/f32[16]...) while((s32[]{:T(128)}, f32[16,80]{1,0:T(8,128)S(1)}, ...), condition=%wide.region_7.9_spmd, body=%wide.region_4.8_spmd.sunk | while | flops 108588 | bytes 96229 | solution.py:122
  191.8 0.8 fusion.146
  200.5 0.8 fusion.146
  209.2 0.8 fusion.146
  217.9 0.8 fusion.146
  226.6 0.8 fusion.146
  235.3 0.8 fusion.146
  244.0 0.8 fusion.146
  252.7 0.8 fusion.146
  261.4 0.8 fusion.146
  270.1 0.8 fusion.146
  278.9 0.8 fusion.146
  287.6 0.8 fusion.146
  296.3 0.8 fusion.146
  305.0 0.8 fusion.146
  313.7 0.8 fusion.146
  322.4 0.8 fusion.146
  323.5 6.7 convolution_bitcast_fusion.8
  330.2 3.3 copy.55
  333.5 1.3 gather_fusion.2
  335.0 140.9 %all-gather.1 = f32[512,4,80]{2,1,0:T(4,128)} all-gather(f32[1,4,80]{2,1,0:T(4,128)S(1)} %convolution_bitcast_fusion.13), channel_id=1, replica_groups=mesh['lat'=16,'lon'=32] {'lat','lon'}, dimensions={0}, use_global_device_ids=true | all-gather | bytes 656640 | tf_op jit(solution)/shard_map/all_gather | solution.py:102
  475.9 1.8 gather_fusion.3
  477.7 141.3 %while.62 = (s32[]{:T(128)}, f32[16,80]{1,0:T(8,128)S(1)}, f32[80,80]{1,0:T(8,128)S(1)}, f32[16,16]{1,0:T(8,128)S(1)}, f32[16]{0:T(128)S(1)}, /*index=5*/f32[16]...) while((s32[]{:T(128)}, f32[16,80]{1,0:T(8,128)S(1)}, ...), condition=%wide.region_11.13_spmd, body=%wide.region_8.12_spmd.sunk | while | flops 108588 | bytes 96229 | solution.py:122
  485.4 0.8 fusion.153
  494.2 0.8 fusion.153
  503.1 0.8 fusion.153
  511.9 0.8 fusion.153
  529.5 0.8 fusion.153
  538.4 0.8 fusion.153
  547.2 0.8 fusion.153
  556.0 0.8 fusion.153
  564.9 0.8 fusion.153
  573.7 0.8 fusion.153
  582.5 0.8 fusion.153
  591.3 0.8 fusion.153
  600.2 0.8 fusion.153
  609.0 0.8 fusion.153
  617.8 0.8 fusion.153
  619.0 3.8 convolution_bitcast_fusion.10
  622.8 4.8 copy.58
  627.7 1.3 gather_fusion.4
  629.1 141.4 %all-gather.2 = f32[512,4,80]{2,1,0:T(4,128)} all-gather(f32[1,4,80]{2,1,0:T(4,128)S(1)} %convolution_bitcast_fusion.12), channel_id=1, replica_groups=mesh['lat'=16,'lon'=32] {'lat','lon'}, dimensions={0}, use_global_device_ids=true | all-gather | bytes 656640 | tf_op jit(solution)/shard_map/all_gather | solution.py:102
  770.5 1.8 gather_fusion.5
  772.3 141.5 %while.63 = (s32[]{:T(128)}, f32[16,80]{1,0:T(8,128)S(1)}, f32[80,80]{1,0:T(8,128)S(1)}, f32[16,16]{1,0:T(8,128)S(1)}, f32[16]{0:T(128)S(1)}, /*index=5*/f32[16]...) while((s32[]{:T(128)}, f32[16,80]{1,0:T(8,128)S(1)}, ...), condition=%wide.region_15.17_spmd, body=%wide.region_12.16_spmd.sunk | while | flops 108588 | bytes 96229 | solution.py:122
  780.1 0.8 fusion.160
  913.8 3.8 convolution_bitcast_fusion.9
  917.7 4.8 copy.61
  922.6 1.3 gather_fusion.6
  924.0 141.2 %all-gather.3 = f32[512,4,80]{2,1,0:T(4,128)} all-gather(f32[1,4,80]{2,1,0:T(4,128)S(1)} %convolution_bitcast_fusion.11), channel_id=1, replica_groups=mesh['lat'=16,'lon'=32] {'lat','lon'}, dimensions={0}, use_global_device_ids=true | all-gather | bytes 656640 | tf_op jit(solution)/shard_map/all_gather | solution.py:102
  1065.1 1.8 gather_fusion.7
  1067.0 141.9 %while.64 = (s32[]{:T(128)}, f32[16,80]{1,0:T(8,128)S(1)}, f32[80,80]{1,0:T(8,128)S(1)}, f32[16,16]{1,0:T(8,128)S(1)}, f32[16]{0:T(128)S(1)}, /*index=5*/f32[16]...) while((s32[]{:T(128)}, f32[16,80]{1,0:T(8,128)S(1)}, ...), condition=%wide.region_19.21_spmd, body=%wide.region_16.20_spmd.sunk | while | flops 108588 | bytes 96229 | solution.py:122
  1208.8 2.3 convolution_convert_fusion
  1211.2 1.4 copy.77
  (742 shorter events, 248.6 us)
Async XLA Ops:
  3.3 10.0 copy-start.2
  3.3 13.1 %copy-start.13 = (s32[4]{0:T(128)S(1)}, s32[4]{0:T(128)}, u32[]{:S(2)}) copy-start(s32[4]{0:T(128)} %param.25) | copy-start | bytes 52
  3.3 16.3 %copy-start.9 = (s32[64]{0:T(128)S(1)}, s32[64]{0:T(128)}, u32[]{:S(2)}) copy-start(s32[64]{0:T(128)} %param.20) | copy-start | bytes 772
  3.3 19.1 %copy-start.10 = (s32[64]{0:T(128)S(1)}, s32[64]{0:T(128)}, u32[]{:S(2)}) copy-start(s32[64]{0:T(128)} %param.21) | copy-start | bytes 772
  3.3 19.2 %copy-start.8 = (f32[2,4,8,128]{3,2,1,0:T(8,128)S(1)}, f32[2,4,8,128]{3,2,1,0:T(8,128)}, u32[]{:S(2)}) copy-start(f32[2,4,8,128]{3,2,1,0:T(8,128)} %param.19) | copy-start | bytes 98308
  3.3 19.3 %copy-start.7 = (s32[64,18]{0,1:T(8,128)S(1)}, s32[64,18]{0,1:T(8,128)}, u32[]{:S(2)}) copy-start(s32[64,18]{0,1:T(8,128)} %param.24) | copy-start | bytes 13828
  3.3 20.1 %copy-start.11 = (f32[64]{0:T(128)S(1)}, f32[64]{0:T(128)}, u32[]{:S(2)}) copy-start(f32[64]{0:T(128)} %param.22) | copy-start | bytes 772
  3.4 20.1 %copy-start.12 = (f32[64]{0:T(128)S(1)}, f32[64]{0:T(128)}, u32[]{:S(2)}) copy-start(f32[64]{0:T(128)} %param.23) | copy-start | bytes 772
  5.6 21.6 %collective-permute-start = (bf16[2,4,80,8,1]{2,3,4,1,0:T(8,128)(2,1)S(1)}, bf16[2,4,80,8,1]{2,3,4,1,0:T(8,128)(2,1)S(1)}, u32[]{:S(2)}, u32[]{:S(2)}) collective-permute-start(bf16[2,4,80,8,1]{2,3,4,1,0:T(8,128)(2,1)S(1)} %copy.73), channel_id=1, source_target_pairs={{0,1},{1,2},{2,3},{3,4},{4,5},{5,6},{6,7},{7,8},{8,9},{9,10},{10,1... | collective-permute-start | bytes 30728 | tf_op jit(solution)/shard_map/ppermute | solution.py:23
  9.4 18.5 %collective-permute-start.1 = (bf16[2,4,80,8,1]{2,3,4,1,0:T(8,128)(2,1)S(1)}, bf16[2,4,80,8,1]{2,3,4,1,0:T(8,128)(2,1)S(1)}, u32[]{:S(2)}, u32[]{:S(2)}) collective-permute-start(bf16[2,4,80,8,1]{2,3,4,1,0:T(8,128)(2,1)S(1)} %copy.74), channel_id=1, source_target_pairs={{1,0},{2,1},{3,2},{4,3},{5,4},{6,5},{7,6},{8,7},{9,8},{10,9},{11,1... | collective-permute-start | bytes 30728 | tf_op jit(solution)/shard_map/ppermute | solution.py:25
  13.7 15.9 %collective-permute-start.2 = (bf16[2,4,80,1,128]{4,2,3,1,0:T(8,128)(2,1)S(1)}, bf16[2,4,80,1,128]{4,2,3,1,0:T(8,128)(2,1)S(1)}, u32[]{:S(2)}, u32[]{:S(2)}) collective-permute-start(bf16[2,4,80,1,128]{4,2,3,1,0:T(8,128)(2,1)S(1)} %copy.75), channel_id=1, source_target_pairs={{0,32},{32,64},{64,96},{96,128},{128,160},{160,192},{192,224},{224... | collective-permute-start | bytes 491528 | tf_op jit(solution)/shard_map/ppermute | solution.py:23
  15.1 14.8 %collective-permute-start.3 = (bf16[2,4,80,1,128]{4,2,3,1,0:T(8,128)(2,1)S(1)}, bf16[2,4,80,1,128]{4,2,3,1,0:T(8,128)(2,1)S(1)}, u32[]{:S(2)}, u32[]{:S(2)}) collective-permute-start(bf16[2,4,80,1,128]{4,2,3,1,0:T(8,128)(2,1)S(1)} %copy.76), channel_id=1, source_target_pairs={{32,0},{64,32},{96,64},{128,96},{160,128},{192,160},{224,192},{256... | collective-permute-start | bytes 491528 | tf_op jit(solution)/shard_map/ppermute | solution.py:25
  19.8 2.8 copy-start.20
  20.4 15.3 %copy-start.3 = (f32[80,80]{1,0:T(8,128)}, f32[80,80]{1,0:T(8,128)S(1)}, u32[]{:S(2)}) copy-start(f32[80,80]{1,0:T(8,128)S(1)} %fusion.31) | copy-start | bytes 76804
  21.1 1.6 copy-start.18
  21.7 1.1 copy-start.16
  22.4 0.5 copy-start.14
  35.8 6.2 copy-start.21
  35.8 6.2 copy-start.34
  35.8 148.4 %copy-start.35 = (f32[16]{0:T(128)S(1)}, f32[16]{0:T(128)}, u32[]{:S(2)}) copy-start(f32[16]{0:T(128)} %get-tuple-element.923) | copy-start | bytes 196
  35.8 148.4 %copy-start.36 = (f32[16]{0:T(128)S(1)}, f32[16]{0:T(128)}, u32[]{:S(2)}) copy-start(f32[16]{0:T(128)} %get-tuple-element.922) | copy-start | bytes 196
  35.8 148.4 %copy-start.37 = (f32[16]{0:T(128)S(1)}, f32[16]{0:T(128)}, u32[]{:S(2)}) copy-start(f32[16]{0:T(128)} %get-tuple-element.924) | copy-start | bytes 196
  330.2 4.6 copy-start.19
  330.2 4.7 copy-start.32
  330.2 147.5 %copy-start.5 = (f32[80,80]{1,0:T(8,128)S(1)}, f32[80,80]{1,0:T(8,128)}, u32[]{:S(2)}) copy-start(f32[80,80]{1,0:T(8,128)} %copy-done.3) | copy-start | bytes 76804
  330.2 147.5 %copy-start.30 = (f32[16]{0:T(128)S(1)}, f32[16]{0:T(128)}, u32[]{:S(2)}) copy-start(f32[16]{0:T(128)} %get-tuple-element.959) | copy-start | bytes 196
  330.2 147.5 %copy-start.31 = (f32[16]{0:T(128)S(1)}, f32[16]{0:T(128)}, u32[]{:S(2)}) copy-start(f32[16]{0:T(128)} %get-tuple-element.958) | copy-start | bytes 196
  330.2 147.5 %copy-start.33 = (f32[16]{0:T(128)S(1)}, f32[16]{0:T(128)}, u32[]{:S(2)}) copy-start(f32[16]{0:T(128)} %get-tuple-element.960) | copy-start | bytes 196
  622.8 6.2 copy-start.17
  622.8 6.2 copy-start.28
  622.8 149.5 %copy-start.6 = (f32[80,80]{1,0:T(8,128)S(1)}, f32[80,80]{1,0:T(8,128)}, u32[]{:S(2)}) copy-start(f32[80,80]{1,0:T(8,128)} %copy-done.3) | copy-start | bytes 76804
  622.8 149.5 %copy-start.26 = (f32[16]{0:T(128)S(1)}, f32[16]{0:T(128)}, u32[]{:S(2)}) copy-start(f32[16]{0:T(128)} %get-tuple-element.995) | copy-start | bytes 196
  622.8 149.5 %copy-start.27 = (f32[16]{0:T(128)S(1)}, f32[16]{0:T(128)}, u32[]{:S(2)}) copy-start(f32[16]{0:T(128)} %get-tuple-element.994) | copy-start | bytes 196
  622.8 149.5 %copy-start.29 = (f32[16]{0:T(128)S(1)}, f32[16]{0:T(128)}, u32[]{:S(2)}) copy-start(f32[16]{0:T(128)} %get-tuple-element.996) | copy-start | bytes 196
  622.8 291.0 %copy-start = (f32[8,80,1024]{2,1,0:T(8,128)S(1)}, f32[8,80,1024]{2,1,0:T(8,128)}, u32[]{:S(2)}) copy-start(f32[8,80,1024]{2,1,0:T(8,128)} %convolution_bitcast_fusion.10) | copy-start | bytes 7864324
  917.7 6.1 copy-start.15
  917.7 6.2 copy-start.24
  917.7 149.3 %copy-start.4 = (f32[80,80]{1,0:T(8,128)S(1)}, f32[80,80]{1,0:T(8,128)}, u32[]{:S(2)}) copy-start(f32[80,80]{1,0:T(8,128)} %copy-done.3) | copy-start | bytes 76804
  917.7 149.3 %copy-start.22 = (f32[16]{0:T(128)S(1)}, f32[16]{0:T(128)}, u32[]{:S(2)}) copy-start(f32[16]{0:T(128)} %get-tuple-element.1031) | copy-start | bytes 196
  917.7 149.3 %copy-start.23 = (f32[16]{0:T(128)S(1)}, f32[16]{0:T(128)}, u32[]{:S(2)}) copy-start(f32[16]{0:T(128)} %get-tuple-element.1030) | copy-start | bytes 196
  917.7 149.3 %copy-start.25 = (f32[16]{0:T(128)S(1)}, f32[16]{0:T(128)}, u32[]{:S(2)}) copy-start(f32[16]{0:T(128)} %get-tuple-element.1032) | copy-start | bytes 196
  917.7 291.1 %copy-start.1 = (f32[8,80,1024]{2,1,0:T(8,128)S(1)}, f32[8,80,1024]{2,1,0:T(8,128)}, u32[]{:S(2)}) copy-start(f32[8,80,1024]{2,1,0:T(8,128)} %convolution_bitcast_fusion.9) | copy-start | bytes 7864324
where the time goes:
time: 1220 us; the launch traced here: 1210 us
  blocking collectives  565 us (46%)
  loops' own time  302 us (25%)
  local copies, waits for them, and re-layouts  159 us (13%)
  other arithmetic  97.6 us (8%)
  matrix products  76.6 us (6%)
    all_gather x4, blocking collectives, per_device(): collected = lax.all_gather(outgoing, ('lat', 'lon'), axis=0, tiled=True)  565 us
    another operation x4, loops' own time, per_device(): lax.fori_loop(0, OBSERVED_BATCH, advance, (prior_values, identity))  302 us
    dot_general x64, matrix products, advance(): turned = jnp.dot(transform_now, weights, precision=HIGHEST_PRECISE)  50.7 us
    reduce_sum x64, other arithmetic, eakf_step(): mean_prior = jnp.mean(prior_row)  39.3 us
    dynamic_slice x64, local copies, waits for them, and re-layouts, advance(): obs_values[obs_index]  38.7 us
    reduce_sum x64, other arithmetic, eakf_step(): spread = jnp.sum(anomaly * anomaly) / (member_list - 1) + EPSILON  38.5 us
    dynamic_slice x64, local copies, waits for them, and re-layouts, advance(): mine_mask[obs_index] * turned[:, None] * increment[None, :]  37.7 us
    dynamic_slice x64, local copies, waits for them, and re-layouts, advance(): obs_errors[obs_index]  37.7 us
  transfers between devices with their start and end apart: 4, of which 0 were waited for; matrix products, arithmetic and copies ran while one was open for 1% of the time, Pallas kernels for 0%

commit v1 on v0

v1 whole, which is shorter than its diff:
```python
import jax
import jax.numpy as jnp
from jax import lax
from jax.experimental import pallas as pl
from jax.experimental.pallas import tpu as pltpu
from jax.sharding import PartitionSpec as P

MESH = pl.DeviceIdType.MESH
EPSILON = 1e-05
MEMBERS = 80
PLANES = 8
LEVELS = 4
CELLS = 1024
NOBS = 64
BATCH = 16
N_LAT = 16
N_LON = 32
N_Z = 16
GROUP = 32
ROWS = PLANES * MEMBERS
F32 = jnp.float32
BF16 = jnp.bfloat16
VM = pltpu.VMEM
SM = pltpu.SMEM


def spec(space):
    return pl.BlockSpec(memory_space=space)


def edges_kernel(prior_ref, rows_ref, cols_ref, wide):
    lane = lax.broadcasted_iota(jnp.int32, (8, 128), 1)

    def plane(p, _):
        def part(g, acc):
            first, last = acc
            base = p * MEMBERS + g * 16
            for i in range(16):
                x = prior_ref[base + i].astype(F32)
                wide[i * 8 : i * 8 + 8, :] = x
                e = g * 16 + i
                first = jnp.where(lane == e, pltpu.roll(x, e, 1), first)
                last = jnp.where(lane == e, pltpu.roll(x, e + 1, 1), last)
            at = pl.multiple_of(base, 16)
            rows_ref[0, pl.ds(at, 16), :] = wide[pl.ds(7, 16, stride=8), :].astype(BF16)
            rows_ref[1, pl.ds(at, 16), :] = wide[pl.ds(0, 16, stride=8), :].astype(BF16)
            return first, last

        zero = jnp.zeros((8, 128), F32)
        first, last = lax.fori_loop(0, 5, part, (zero, zero))
        cols_ref[0, p] = last.astype(BF16)
        cols_ref[1, p] = first.astype(BF16)
        return 0

    lax.fori_loop(0, PLANES, plane, 0)


def halo_kernel(rows_ref, cols_ref, rows_out, cols_out, send_sem, recv_sem):
    lat = lax.axis_index("lat")
    lon = lax.axis_index("lon")
    north = (lax.rem(lat + 1, N_LAT), lon)
    south = (lax.rem(lat + N_LAT - 1, N_LAT), lon)
    east = (lat, lax.rem(lon + 1, N_LON))
    west = (lat, lax.rem(lon + N_LON - 1, N_LON))
    barrier = pltpu.get_barrier_semaphore()
    for peer in (north, south, east, west):
        pl.semaphore_signal(barrier, inc=1, device_id=peer, device_id_type=MESH)
    pl.semaphore_wait(barrier, 4)
    copies = []
    for n, (src, dst, peer) in enumerate(
        (
            (rows_ref.at[0], rows_out.at[0], north),
            (rows_ref.at[1], rows_out.at[1], south),
            (cols_ref.at[0], cols_out.at[0], east),
            (cols_ref.at[1], cols_out.at[1], west),
        )
    ):
        copy = pltpu.make_async_remote_copy(
            src_ref=src,
            dst_ref=dst,
            send_sem=send_sem.at[n],
            recv_sem=recv_sem.at[n],
            device_id=peer,
            device_id_type=MESH,
        )
        copy.start()
        copies.append(copy)
    for copy in copies:
        copy.wait()


def forecast_kernel(
    me_ref, tile_ref, site_ref, order_ref, prior_ref, wind_ref, rows_ref, cols_ref, f_ref, obs_ref
):
    me = me_ref[0]
    lat = me // N_LON
    lane = lax.broadcasted_iota(jnp.int32, (8, 128), 1)
    sub = lax.broadcasted_iota(jnp.int32, (8, 128), 0)
    has_south = (lat > 0).astype(F32)
    has_north = (lat < N_LAT - 1).astype(F32)

    def plane(p, _):
        level = lax.rem(p, LEVELS)
        cu = wind_ref[level]
        cv = wind_ref[LEVELS + level]
        cu_up, cu_dn = jnp.maximum(cu, 0.0), jnp.minimum(cu, 0.0)
        cv_up, cv_dn = jnp.maximum(cv, 0.0), jnp.minimum(cv, 0.0)
        from_west = cols_ref[0, p].astype(F32)
        from_east = cols_ref[1, p].astype(F32)

        def part(g, _):
            base = p * MEMBERS + g * 16
            at = pl.multiple_of(base, 16)
            south_rows = rows_ref[0, pl.ds(at, 16), :].astype(F32) * has_south
            north_rows = rows_ref[1, pl.ds(at, 16), :].astype(F32) * has_north
            for i in range(16):
                e = g * 16 + i
                x = prior_ref[base + i].astype(F32)
                xw = jnp.where(lane == 0, pltpu.roll(from_west, 128 - e, 1), pltpu.roll(x, 1, 1))
                xe = jnp.where(
                    lane == 127, pltpu.roll(from_east, 127 - e, 1), pltpu.roll(x, 127, 1)
                )
                xs = jnp.where(sub == 0, south_rows[i : i + 1, :], pltpu.roll(x, 1, 0))
                xn = jnp.where(sub == 7, north_rows[i : i + 1, :], pltpu.roll(x, 7, 0))
                f = (
                    x
                    - cu_up * (x - xw)
                    - cu_dn * (xe - x)
                    - cv_up * (x - xs)
                    - cv_dn * (xn - x)
                )
                f_ref[pl.ds(pl.multiple_of((base + i) * 8, 8), 8), :] = f
            return 0

        lax.fori_loop(0, 5, part, 0)
        return 0

    lax.fori_loop(0, PLANES, plane, 0)
    obs_ref[...] = jnp.zeros(obs_ref.shape, F32)

    def one(q, _):
        k = order_ref[q // BATCH] * BATCH + lax.rem(q, BATCH)

        @pl.when(tile_ref[k] == me)
        def _():
            s = site_ref[k]
            p = s // CELLS
            r = lax.rem(s, CELLS) // 128
            c = lax.rem(s, 128)
            cells = f_ref[pl.ds(p * (MEMBERS * 8) + r, MEMBERS, stride=8), :]
            cells = jnp.concatenate([cells, jnp.zeros((128 - MEMBERS, 128), F32)], axis=0)
            pick = (lane == c).astype(F32)
            row = lax.dot_general(
                pick,
                cells,
                (((1,), (1,)), ((), ())),
                precision=lax.Precision.HIGHEST,
                preferred_element_type=F32,
            )
            obs_ref[q // 2, pl.ds(lax.rem(q, 2), 1), :] = row[0:1, :]

        return 0

    lax.fori_loop(0, NOBS, one, 0)


def exchange_kernel(
    obs_ref, out_ref, got1, part, got2, total, got3, send1, recv1, send2, recv2, send3, recv3
):
    lat = lax.axis_index("lat")
    lon = lax.axis_index("lon")
    z = lon // 2
    core = lax.rem(lon, 2)
    mine = lat * 2 + core

    def group_id(n):
        return (n // 2, z * 2 + lax.rem(n, 2))

    def other(d):
        return lax.rem(mine + d, GROUP)

    def other_z(d):
        return lax.rem(z + d, N_Z)

    barrier = pltpu.get_barrier_semaphore()

    def greet(d, _):
        pl.semaphore_signal(barrier, inc=1, device_id=group_id(other(d)), device_id_type=MESH)
        return 0

    def greet_z(d, _):
        pl.semaphore_signal(
            barrier, inc=1, device_id=(lat, other_z(d) * 2 + core), device_id_type=MESH
        )
        return 0

    lax.fori_loop(1, N_Z, greet_z, 0)
    lax.fori_loop(1, GROUP, greet, 0)
    pl.semaphore_wait(barrier, GROUP - 1 + N_Z - 1)

    def copy1(dst, src_slot):
        return pltpu.make_async_remote_copy(
            src_ref=obs_ref.at[dst],
            dst_ref=got1.at[src_slot],
            send_sem=send1.at[dst],
            recv_sem=recv1.at[src_slot],
            device_id=group_id(dst),
            device_id_type=MESH,
        )

    def copy2(dst, src_slot):
        return pltpu.make_async_remote_copy(
            src_ref=part,
            dst_ref=got2.at[src_slot],
            send_sem=send2.at[dst],
            recv_sem=recv2.at[src_slot],
            device_id=(lat, dst * 2 + core),
            device_id_type=MESH,
        )

    def copy3(dst, src_slot):
        return pltpu.make_async_remote_copy(
            src_ref=total,
            dst_ref=got3.at[src_slot],
            send_sem=send3.at[dst],
            recv_sem=recv3.at[src_slot],
            device_id=group_id(dst),
            device_id_type=MESH,
        )

    def loop(first, count, body):
        lax.fori_loop(first, count, lambda d, c: (body(d), c)[1], 0)

    loop(1, GROUP, lambda d: copy1(other(d), mine).start())

    def take1(d, acc):
        src = other(d)
        copy1(src, src).wait_recv()
        return acc + got1[src]

    part[...] = lax.fori_loop(1, GROUP, take1, obs_ref[mine])
    loop(1, N_Z, lambda d: copy2(other_z(d), z).start())

    def take2(d, acc):
        src = other_z(d)
        copy2(src, src).wait_recv()
        return acc + got2[src]

    total[...] = lax.fori_loop(1, N_Z, take2, part[...])
    loop(1, GROUP, lambda d: copy3(other(d), mine).start())
    out_ref[mine] = total[...]

    def take3(d):
        src = other(d)
        copy3(src, src).wait_recv()
        out_ref[src] = got3[src]

    loop(1, GROUP, take3)
    loop(1, GROUP, lambda d: copy1(other(d), mine).wait_send())
    loop(1, N_Z, lambda d: copy2(other_z(d), z).wait_send())
    loop(1, GROUP, lambda d: copy3(other(d), mine).wait_send())


def filter_kernel(
    me_ref,
    tile_ref,
    order_ref,
    value_ref,
    var_ref,
    bits_s_ref,
    bits_ref,
    obs_ref,
    f_ref,
    out_ref,
    table,
    mask_ref,
    turned,
):
    me = me_ref[0]
    for n in range(GROUP):
        table[2 * n : 2 * n + 2, :] = obs_ref[n]
    table[NOBS:, :] = jnp.zeros((128 - NOBS, 128), F32)
    lane = lax.broadcasted_iota(jnp.int32, (1, 128), 1)

    def put(q, row):
        k = order_ref[q // BATCH] * BATCH + lax.rem(q, BATCH)
        return jnp.where(lane == q, tile_ref[k], row)

    owners = lax.fori_loop(0, NOBS, put, jnp.zeros((1, 128), jnp.int32))
    word_of = owners // 30
    bit_of = owners - word_of * 30
    words = bits_ref[...]
    chosen = jnp.zeros((NOBS, 128), jnp.int32)
    for w in range(18):
        chosen = jnp.where(word_of == w, words[:, w : w + 1], chosen)
    mask_ref[...] = jnp.bitwise_and(jnp.right_shift(chosen, bit_of), 1).astype(F32)

    own_word = me // 30
    own_bit = lax.rem(me, 30)
    state = jnp.transpose(table[...])[:MEMBERS, :]
    means = jnp.sum(state, axis=0, keepdims=True) * (1.0 / MEMBERS)
    anomalies = state - means
    eye = (
        lax.broadcasted_iota(jnp.int32, (MEMBERS, 128), 0)
        == lax.broadcasted_iota(jnp.int32, (MEMBERS, 128), 1)
    ).astype(F32)

    def batch(b, carry):
        anomalies, means, turn = carry
        base = order_ref[b] * BATCH
        for j in range(BATCH):
            k = base + j
            r = var_ref[k]
            val = value_ref[k]
            own = jnp.bitwise_and(jnp.right_shift(bits_s_ref[k, own_word], own_bit), 1)
            own = own.astype(F32) * (1.0 / (MEMBERS - 1))
            row = mask_ref[pl.ds(k, 1), :] * (1.0 / (MEMBERS - 1))
            a = jnp.broadcast_to(anomalies[:, j : j + 1], (MEMBERS, 128))
            m = jnp.broadcast_to(means[:, j : j + 1], (1, 128))
            v = jnp.sum(a * a, axis=0, keepdims=True) * (1.0 / (MEMBERS - 1)) + EPSILON
            cov = jnp.sum(anomalies * a, axis=0, keepdims=True) * row
            cov_own = jnp.sum(turn * a, axis=0, keepdims=True) * own
            whole = v + r
            shrink = 1.0 / (whole + jnp.sqrt(r * whole))
            shift = (val - m) / whole
            anomalies = anomalies - (cov * shrink) * a
            means = means + cov * shift
            turn = turn + cov_own * (shift - shrink * a)
        mask_ref[...] = pltpu.roll(mask_ref[...], 128 - BATCH, 1)
        return (
            pltpu.roll(anomalies, 128 - BATCH, 1),
            pltpu.roll(means, 128 - BATCH, 1),
            turn,
        )

    _, _, turn = lax.fori_loop(0, NOBS // BATCH, batch, (anomalies, means, eye))
    high = turn.astype(BF16).astype(F32)
    low = (turn - high)[:, :MEMBERS]
    high = high[:, :MEMBERS]
    left = jnp.concatenate([high, high, low], axis=1).astype(BF16)

    def plane(p, _):
        start = p * (MEMBERS * 8)
        blocks = []
        for r in range(8):
            x = f_ref[pl.ds(start + r, MEMBERS, stride=8), :]
            big = x.astype(BF16)
            small = (x - big.astype(F32)).astype(BF16)
            blocks.append(jnp.concatenate([big, small, big], axis=0))
        for h in range(4):
            right = jnp.concatenate(blocks[2 * h : 2 * h + 2], axis=1)
            result = jnp.dot(left, right, preferred_element_type=F32)
            for i in range(2):
                turned[pl.ds(2 * h + i, MEMBERS, stride=8), :] = result[:, 128 * i : 128 * i + 128]
        out_ref[pl.ds(p * MEMBERS, MEMBERS)] = (
            turned[...].reshape(MEMBERS, 8, 128).astype(BF16)
        )
        return 0

    lax.fori_loop(0, PLANES, plane, 0)


def per_device(prior_state, courant, obs_tile, obs_site, obs_value, obs_var, loc_bits, batch_order):
    prior = prior_state.reshape(ROWS, 8, 128)
    wind = courant.reshape(2 * LEVELS, 8, 128)
    me = (lax.axis_index("lat") * N_LON + lax.axis_index("lon")).astype(jnp.int32)[None]
    dma = pltpu.SemaphoreType.DMA
    rows_shape = jax.ShapeDtypeStruct((2, ROWS, 128), BF16)
    cols_shape = jax.ShapeDtypeStruct((2, PLANES, 8, 128), BF16)
    obs_shape = jax.ShapeDtypeStruct((GROUP, 2, 128), F32)
    edge_rows, edge_cols = pl.pallas_call(
        edges_kernel,
        out_shape=(rows_shape, cols_shape),
        in_specs=[spec(VM)],
        out_specs=(spec(VM), spec(VM)),
        scratch_shapes=[VM((128, 128), F32)],
        name="edges",
    )(prior)
    halo_rows, halo_cols = pl.pallas_call(
        halo_kernel,
        out_shape=(rows_shape, cols_shape),
        in_specs=[spec(VM)] * 2,
        out_specs=(spec(VM), spec(VM)),
        scratch_shapes=[dma((4,)), dma((4,))],
        compiler_params=pltpu.CompilerParams(collective_id=0, has_side_effects=True),
        name="halo",
    )(edge_rows, edge_cols)
    forecast, contribution = pl.pallas_call(
        forecast_kernel,
        out_shape=(jax.ShapeDtypeStruct((ROWS * 8, 128), F32), obs_shape),
        in_specs=[spec(SM)] * 4 + [spec(VM)] * 4,
        out_specs=(spec(VM), spec(VM)),
        name="forecast",
    )(me, obs_tile, obs_site, batch_order, prior, wind, halo_rows, halo_cols)
    observed = pl.pallas_call(
        exchange_kernel,
        out_shape=obs_shape,
        in_specs=[spec(VM)],
        out_specs=spec(VM),
        scratch_shapes=[
            VM((GROUP, 2, 128), F32),
            VM((2, 128), F32),
            VM((N_Z, 2, 128), F32),
            VM((2, 128), F32),
            VM((GROUP, 2, 128), F32),
            dma((GROUP,)),
            dma((GROUP,)),
            dma((N_Z,)),
            dma((N_Z,)),
            dma((GROUP,)),
            dma((GROUP,)),
        ],
        compiler_params=pltpu.CompilerParams(collective_id=1, has_side_effects=True),
        name="exchange",
    )(contribution)
    bits = jnp.pad(loc_bits, ((0, 0), (0, 128 - loc_bits.shape[1])))
    analysis = pl.pallas_call(
        filter_kernel,
        out_shape=jax.ShapeDtypeStruct((ROWS, 8, 128), BF16),
        in_specs=[spec(SM)] * 6 + [spec(VM)] * 3,
        out_specs=spec(VM),
        scratch_shapes=[VM((128, 128), F32), VM((NOBS, 128), F32), VM((MEMBERS * 8, 128), F32)],
        name="filter",
    )(me, obs_tile, batch_order, obs_value, obs_var, loc_bits, bits, observed, forecast)
    return analysis.reshape(prior_state.shape)


def solution(mesh):
    placed = (
        P(None, None, None, "lat", "lon"),
        P(None, None, "lat", "lon"),
        P(),
        P(),
        P(),
        P(),
        P(),
        P(),
    )
    return jax.shard_map(
        per_device,
        mesh=mesh,
        in_specs=placed,
        out_specs=P(None, None, None, "lat", "lon"),
        check_vma=False,
    )
```

time: 1220 us -> 78.5 us (0.06)
  blocking collectives: 565 us -> 0 us
  loops' own time: 302 us -> 0 us
  local copies, waits for them, and re-layouts: 159 us -> 1.42 us
  other arithmetic: 97.6 us -> 0 us
  Pallas kernels: 0 us -> 76.7 us
  matrix products: 76.6 us -> 0 us
    all_gather x4 -> x0, blocking collectives: 565 us -> none  [per_device(): collected = lax.all_gather(outgoing, ('lat', 'lon'), axis=0, tiled=True)]
    another operation x4 -> x0, loops' own time: 302 us -> none  [per_device(): lax.fori_loop(0, OBSERVED_BATCH, advance, (prior_values, identity))]
    dynamic_slice x195 -> x0, local copies, waits for them, and re-layouts: 116 us -> none  [the longest x64 38.7 us: advance(): obs_values[obs_index]]
    reduce_sum x132 -> x0, other arithmetic: 78.2 us -> none  [the longest x64 39.3 us: eakf_step(): mean_prior = jnp.mean(prior_row)]
    pallas_call x0 -> x5, Pallas kernels: none -> 76.7 us  [the longest x1 34.1 us: per_device(): pl.pallas_call(exchange_kernel, out_shape=obs_shape, in_specs=[spec(VM)],...]
    dot_general x136 -> x0, matrix products: 76.6 us -> none  [the longest x64 50.7 us: advance(): turned = jnp.dot(transform_now, weights, precision=HIGHEST_PRECISE)]
    gather x12 -> x0, local copies, waits for them, and re-layouts: 13.3 us -> none  [the longest x4 5.93 us: per_device(): prior_values = collected[owner_tiles * CAP + slot_rank]]
    transpose x3 -> x0, local copies, waits for them, and re-layouts: 13 us -> none  [per_device(): jnp.einsum('pec,eg->pgc', current_state, transform_now, precision=HIGHEST...]
  transfers between devices with their start and end apart: 4 -> 0, of which waited for: 0 -> 0; matrix products, arithmetic and copies ran while one was open for 1% -> 0% of each run, Pallas kernels for 0% -> 0%
where the time goes in v1:
time: 78.5 us; the launch traced here: 78.1 us
  Pallas kernels  76.7 us (98%)
  local copies, waits for them, and re-layouts  1.42 us (2%)
    pallas_call x1, Pallas kernels, per_device(): pl.pallas_call(exchange_kernel, out_shape=obs_shape, in_specs=[spec(VM)],...  34.1 us
    pallas_call x1, Pallas kernels, per_device(): pl.pallas_call(filter_kernel, out_shape=jax.ShapeDtypeStruct((ROWS, 8, 12...  14.3 us
    pallas_call x1, Pallas kernels, per_device(): pl.pallas_call(halo_kernel, out_shape=(rows_shape, cols_shape), in_specs=...  13.6 us
    pallas_call x1, Pallas kernels, per_device(): pl.pallas_call(forecast_kernel, out_shape=(jax.ShapeDtypeStruct((ROWS * 8...  9.05 us
    pallas_call x1, Pallas kernels, per_device(): pl.pallas_call(edges_kernel, out_shape=(rows_shape, cols_shape), in_specs...  5.7 us

profile of v1, /device:TPU:1, one launch (start us, length us, event | category | flops | bytes accessed | tf_op | source)
XLA Modules:
  0.0 78.1 jit_solution(4224762636257401694)
XLA Ops:
  0.0 0.8 %copy.10.bits_s_ref = s32[64,18]{1,0:T(8,128)S(1)} copy(s32[64,18]{0,1:T(8,128)} %param.14) | data formatting | bytes 9216 | tf_op args[6]
  0.8 0.0 copy-start
  0.8 0.6 pad.4.bits_ref
  1.4 5.7 %edges.1 = (bf16[2,640,128]{2,1,0:T(8,128)(2,1)}, bf16[2,8,8,128]{3,2,1,0:T(8,128)(2,1)}) custom-call(bf16[640,8,128]{2,1,0:T(8,128)(2,1)} %bitcast.4), custom_call_target="tpu_custom_call" | custom-call | tf_op jit(solution)/shard_map/edges/pallas_call | solution.py:371
  7.1 13.6 %halo.1 = (bf16[2,640,128]{2,1,0:T(8,128)(2,1)}, bf16[2,8,8,128]{3,2,1,0:T(8,128)(2,1)}) custom-call(bf16[2,640,128]{2,1,0:T(8,128)(2,1)} %get-tuple-element.11.rows_ref, bf16[2,8,8,128]{3,2,1,0:T(8,128)(2,1)} %get-tuple-element.12.cols_ref), custom_call_target="tpu_custom_call" | custom-call | tf_op jit(solution)/shard_map/halo/pallas_call | solution.py:379
  20.7 9.1 %forecast.1 = (f32[5120,128]{1,0:T(8,128)}, f32[32,2,128]{2,1,0:T(2,128)}) custom-call(s32[1]{0:T(128)} %bitcast.me_ref, s32[64]{0:T(128)} %tile_ref.3, s32[64]{0:T(128)} %site_ref.1, s32[4]{0:T(128)} %order_ref.3, bf16[640,8,128]{2,1,0:T(8,128)(2,1)} %bitcast.5, f32[8,8,128]{2,1,0:T(8,128)} %bitcast.6, bf16[2,640,128]{2,1,0:T(8,128)(2,1)} %get-tuple-element.13.rows_ref, ...), custom_call_target="tpu_custom_call" | custom-call | tf_op jit(solution)/shard_map/forecast/pallas_call | solution.py:388
  29.7 0.0 copy-done
  29.7 34.1 %exchange.1.obs_ref = f32[32,2,128]{2,1,0:T(2,128)} custom-call(f32[32,2,128]{2,1,0:T(2,128)} %get-tuple-element.15.obs_ref), custom_call_target="tpu_custom_call" | custom-call | tf_op jit(solution)/shard_map/exchange/pallas_call | solution.py:395
  63.8 14.3 %filter.1 = bf16[640,8,128]{2,1,0:T(8,128)(2,1)} custom-call(s32[1]{0:T(128)} %bitcast.me_ref, s32[64]{0:T(128)} %tile_ref.3, s32[4]{0:T(128)} %order_ref.3, f32[64]{0:T(128)} %value_ref.1, f32[64]{0:T(128)} %var_ref.1, s32[64,18]{1,0:T(8,128)} %copy-done, s32[64,128]{1,0:T(8,128)} %pad.4.bits_ref, f32[32,2,128]{2,1,0:T(2,128)} %exchange.1.obs_ref, ...), custom_call_target="tpu_custom_call" | custom-call | tf_op jit(solution)/shard_map/filter/pallas_call | solution.py:417
Async XLA Ops:
  0.8 29.0 %copy-start = (s32[64,18]{1,0:T(8,128)}, s32[64,18]{1,0:T(8,128)S(1)}, u32[]{:S(2)}) copy-start(s32[64,18]{1,0:T(8,128)S(1)} %copy.10.bits_s_ref) | copy-start | bytes 13828

commit v2 on v1

v2 whole, which is shorter than its diff:
```python
import jax
import jax.numpy as jnp
from jax import lax
from jax.experimental import pallas as pl
from jax.experimental.pallas import tpu as pltpu
from jax.sharding import PartitionSpec as P

MESH = pl.DeviceIdType.MESH
EPSILON = 1e-05
MEMBERS = 80
PLANES = 8
LEVELS = 4
CELLS = 1024
NOBS = 64
BATCH = 16
N_LAT = 16
N_LON = 32
N_Z = 16
GROUP = 32
ROWS = PLANES * MEMBERS
F32 = jnp.float32
BF16 = jnp.bfloat16
VM = pltpu.VMEM
SM = pltpu.SMEM


def spec(space):
    return pl.BlockSpec(memory_space=space)


def exchange_kernel(
    tile_ref,
    site_ref,
    order_ref,
    prior_ref,
    wind_ref,
    f_ref,
    out_ref,
    wide,
    rows,
    edge_cols,
    halo_cols,
    mine_obs,
    got1,
    part,
    got2,
    total,
    halo_send,
    halo_recv,
    send,
    recv,
):
    lat = lax.axis_index("lat")
    lon = lax.axis_index("lon")
    z = lon // 2
    core = lax.rem(lon, 2)
    mine = lat * 2 + core
    me = lat * N_LON + lon
    north = (lax.rem(lat + 1, N_LAT), lon)
    south = (lax.rem(lat + N_LAT - 1, N_LAT), lon)
    east = (lat, lax.rem(lon + 1, N_LON))
    west = (lat, lax.rem(lon + N_LON - 1, N_LON))
    lane = lax.broadcasted_iota(jnp.int32, (8, 128), 1)
    sub = lax.broadcasted_iota(jnp.int32, (8, 128), 0)

    def other(d):
        return lax.rem(mine + d, GROUP)

    def group_id(n):
        return (n // 2, z * 2 + lax.rem(n, 2))

    def z_step(n):
        return 8 + ((n + 1) // 2) * (2 * lax.rem(n + 1, 2) - 1)

    def z_id(d):
        return (lat, lax.rem(z + d, N_Z) * 2 + core)

    def loop(first, count, body):
        lax.fori_loop(first, count, lambda d, c: (body(d), c)[1], 0)

    barrier = pltpu.get_barrier_semaphore()

    def greet(peer):
        pl.semaphore_signal(barrier, inc=1, device_id=peer, device_id_type=MESH)

    loop(0, N_Z - 1, lambda n: greet(z_id(z_step(n))))
    loop(1, GROUP, lambda d: greet(group_id(other(d))))
    greet(east)
    greet(west)

    lanes = lax.broadcasted_iota(jnp.int32, (MEMBERS, 128), 1)

    def edge_plane(p, acc):
        def block(g):
            for i in range(16):
                at = pl.multiple_of(g * 128 + i * 8, 8)
                wide[pl.ds(at, 8), :] = prior_ref[p * MEMBERS + g * 16 + i].astype(F32)
            for r in range(8):
                part_rows = wide[pl.ds(g * 128 + r, 16, stride=8), :]
                rows[p, r + 1, pl.ds(pl.multiple_of(g * 16, 16), 16), :] = part_rows.astype(BF16)

        loop(0, 5, block)
        first, last = acc
        for r in range(8):
            x = rows[p, r + 1].astype(F32)
            here = lanes == p * 8 + r
            first = jnp.where(here, pltpu.roll(x, p * 8 + r, 1), first)
            last = jnp.where(here, pltpu.roll(x, p * 8 + r + 1, 1), last)
        return first, last

    zero = jnp.zeros((MEMBERS, 128), F32)
    first, last = lax.fori_loop(0, PLANES, edge_plane, (zero, zero))
    edge_cols[0] = last.astype(BF16)
    edge_cols[1] = first.astype(BF16)

    halves = []
    for h in range(2):
        owned = jnp.int32(0)
        for n in range(32):
            q = 32 * h + n
            k = order_ref[q // BATCH] * BATCH + q % BATCH
            hit = (tile_ref[k] == me).astype(jnp.int32)
            owned = owned | (hit << n)
        halves.append(owned)

    pl.semaphore_wait(barrier, GROUP - 1 + N_Z - 1 + 2)
    halos = []
    for n, (src, dst, peer) in enumerate(
        (
            (rows.at[:, 8], rows.at[:, 0], north),
            (rows.at[:, 1], rows.at[:, 9], south),
            (edge_cols.at[0], halo_cols.at[0], east),
            (edge_cols.at[1], halo_cols.at[1], west),
        )
    ):
        copy = pltpu.make_async_remote_copy(
            src_ref=src,
            dst_ref=dst,
            send_sem=halo_send.at[n],
            recv_sem=halo_recv.at[n],
            device_id=peer,
            device_id_type=MESH,
        )
        copy.start()
        halos.append(copy)
    for copy in halos:
        copy.wait_recv()

    has_south = (lat > 0).astype(F32)
    has_north = (lat < N_LAT - 1).astype(F32)
    for p in range(PLANES):
        rows[p, 0] = (rows[p, 0].astype(F32) * has_south).astype(BF16)
        rows[p, 9] = (rows[p, 9].astype(F32) * has_north).astype(BF16)
    fill = jnp.zeros((128 - MEMBERS, 128), BF16)
    place = lax.broadcasted_iota(jnp.int32, (NOBS, 128), 0)

    def slot(n, carry):
        lo, hi, table = carry
        use_hi = lo == 0
        word = jnp.where(use_hi, hi, lo)
        low = word & (-word)
        q = jnp.int32(0)
        for bit, pattern in enumerate(
            (-1431655766, -858993460, -252645136, -16711936, -65536)
        ):
            q = q + jnp.where((low & jnp.int32(pattern)) != 0, 1 << bit, 0)
        q = q + jnp.where(use_hi, 32, 0)
        spot = jnp.where(word == 0, NOBS, q)
        lo_next = jnp.where(use_hi, lo, lo & (lo - 1))
        hi_next = jnp.where(use_hi, hi & (hi - 1), hi)
        k = order_ref[q // BATCH] * BATCH + q % BATCH
        s = site_ref[k]
        p = s // CELLS
        r = (s // 128) % 8
        c = s % 128
        around = jnp.concatenate(
            [rows[p, r + 1], fill, rows[p, r], fill, rows[p, r + 2], fill], axis=0
        )
        shift = jnp.where(sub == 1, -1, jnp.where(sub == 2, 1, 0))
        pick = (lane == c + shift).astype(BF16)
        found = lax.dot_general(
            pick, around, (((1,), (1,)), ((), ())), preferred_element_type=F32
        )
        sides = jnp.concatenate([halo_cols[0], fill, halo_cols[1], fill], axis=0)
        beside = lax.dot_general(
            (lane == p * 8 + r).astype(BF16),
            sides,
            (((1,), (1,)), ((), ())),
            preferred_element_type=F32,
        )
        at_cell = (sub == r) & (lane == c)
        level = p % LEVELS
        cu = jnp.sum(jnp.where(at_cell, wind_ref[level], 0.0), axis=0, keepdims=True)
        cv = jnp.sum(jnp.where(at_cell, wind_ref[LEVELS + level], 0.0), axis=0, keepdims=True)
        cu = jnp.sum(cu, axis=1, keepdims=True)
        cv = jnp.sum(cv, axis=1, keepdims=True)
        x = found[0:1, 0:128]
        column = jnp.full((1, 128), c, jnp.int32)
        xw = jnp.where(column == 0, beside[0:1, 0:128], found[1:2, 0:128])
        xe = jnp.where(column == 127, beside[0:1, 128:256], found[2:3, 0:128])
        xs = found[0:1, 128:256]
        xn = found[0:1, 256:384]
        f = (
            x
            - jnp.maximum(cu, 0.0) * (x - xw)
            - jnp.minimum(cu, 0.0) * (xe - x)
            - jnp.maximum(cv, 0.0) * (x - xs)
            - jnp.minimum(cv, 0.0) * (xn - x)
        )
        table = jnp.where(place == spot, f, table)
        return lo_next, hi_next, table

    _, _, table = lax.fori_loop(
        0, BATCH, slot, (halves[0], halves[1], jnp.zeros((NOBS, 128), F32))
    )
    for n in range(GROUP):
        mine_obs[n] = table[2 * n : 2 * n + 2, :]

    def copy1(dst, slot_id):
        return pltpu.make_async_remote_copy(
            src_ref=mine_obs.at[dst],
            dst_ref=got1.at[slot_id],
            send_sem=send.at[0],
            recv_sem=recv.at[0],
            device_id=group_id(dst),
            device_id_type=MESH,
        )

    def copy2(d):
        return pltpu.make_async_remote_copy(
            src_ref=part,
            dst_ref=got2.at[d],
            send_sem=send.at[1],
            recv_sem=recv.at[1],
            device_id=z_id(d),
            device_id_type=MESH,
        )

    def copy3(dst):
        return pltpu.make_async_remote_copy(
            src_ref=total,
            dst_ref=out_ref.at[mine],
            send_sem=send.at[2],
            recv_sem=recv.at[2],
            device_id=group_id(dst),
            device_id_type=MESH,
        )

    def bulk(buffer, count, n):
        return pltpu.make_async_remote_copy(
            src_ref=buffer.at[pl.ds(0, count)],
            dst_ref=buffer.at[pl.ds(0, count)],
            send_sem=send.at[n],
            recv_sem=recv.at[n],
            device_id=north,
            device_id_type=MESH,
        )

    lane16 = lax.broadcasted_iota(jnp.int32, (16, 128), 1)

    def forecast(p):
        level = lax.rem(p, LEVELS)
        for r in range(8):
            cu = wind_ref[level, r : r + 1, :]
            cv = wind_ref[LEVELS + level, r : r + 1, :]
            cu_up, cu_dn = jnp.maximum(cu, 0.0), jnp.minimum(cu, 0.0)
            cv_up, cv_dn = jnp.maximum(cv, 0.0), jnp.minimum(cv, 0.0)
            spot = p * 8 + r
            cells = slice(128 * r, 128 * r + 128)
            for g in range(5):
                some = slice(16 * g, 16 * g + 16)
                x = rows[p, r + 1, some, :].astype(F32)
                xs = rows[p, r, some, :].astype(F32)
                xn = rows[p, r + 2, some, :].astype(F32)
                from_west = halo_cols[0, some, :].astype(F32)
                from_east = halo_cols[1, some, :].astype(F32)
                xw = jnp.where(
                    lane16 == 0,
                    pltpu.roll(from_west, lax.rem(128 - spot, 128), 1),
                    pltpu.roll(x, 1, 1),
                )
                xe = jnp.where(
                    lane16 == 127, pltpu.roll(from_east, 127 - spot, 1), pltpu.roll(x, 127, 1)
                )
                f = (
                    x
                    - cu_up * (x - xw)
                    - cu_dn * (xe - x)
                    - cv_up * (x - xs)
                    - cv_dn * (xn - x)
                )
                big = f.astype(BF16)
                f_ref[p, some, cells] = big
                low = slice(MEMBERS + 16 * g, MEMBERS + 16 * g + 16)
                f_ref[p, low, cells] = (f - big.astype(F32)).astype(BF16)

    loop(1, GROUP, lambda d: copy1(other(d), d).start())
    loop(0, 2, forecast)
    bulk(got1, GROUP - 1, 0).wait_recv()
    acc = mine_obs[mine]
    for d in range(1, GROUP):
        acc = acc + got1[d]
    part[...] = acc
    loop(0, N_Z - 1, lambda n: copy2(z_step(n)).start())
    loop(2, 6, forecast)
    bulk(got2, N_Z - 1, 1).wait_recv()
    acc = part[...]
    for d in range(1, N_Z):
        acc = acc + got2[d]
    total[...] = acc
    loop(1, GROUP, lambda d: copy3(other(d)).start())
    out_ref[mine] = acc
    loop(6, PLANES, forecast)
    bulk(out_ref, GROUP - 1, 2).wait_recv()
    for copy in halos:
        copy.wait_send()
    bulk(got1, GROUP - 1, 0).wait_send()
    bulk(got2, N_Z - 1, 1).wait_send()
    bulk(got1, GROUP - 1, 2).wait_send()


def filter_kernel(
    me_ref,
    tile_ref,
    order_ref,
    value_ref,
    var_ref,
    bits_ref,
    obs_ref,
    f_ref,
    out_ref,
    table,
    mask_ref,
    own_ref,
    turned,
):
    me = me_ref[0]
    for n in range(GROUP):
        table[2 * n : 2 * n + 2, :] = obs_ref[n]
    table[NOBS:, :] = jnp.zeros((128 - NOBS, 128), F32)
    lane = lax.broadcasted_iota(jnp.int32, (1, 128), 1)

    def put(q, row):
        k = order_ref[q // BATCH] * BATCH + lax.rem(q, BATCH)
        return jnp.where(lane == q, tile_ref[k], row)

    owners = lax.fori_loop(0, NOBS, put, jnp.zeros((1, 128), jnp.int32))
    word_of = owners // 30
    bit_of = owners - word_of * 30
    own_word = me // 30
    words = bits_ref[...]
    chosen = jnp.zeros((NOBS, 128), jnp.int32)
    chosen_own = jnp.zeros((NOBS, 128), jnp.int32)
    for w in range(18):
        word = jnp.broadcast_to(words[:, w : w + 1], (NOBS, 128))
        chosen = jnp.where(word_of == w, word, chosen)
        chosen_own = jnp.where(own_word == w, word, chosen_own)
    scale = 1.0 / (MEMBERS - 1)
    mask_ref[...] = jnp.bitwise_and(jnp.right_shift(chosen, bit_of), 1).astype(F32) * scale
    own_bit = jnp.full((NOBS, 128), lax.rem(me, 30), jnp.int32)
    own_ref[...] = jnp.bitwise_and(jnp.right_shift(chosen_own, own_bit), 1).astype(F32) * scale
    state = jnp.transpose(table[...])[:MEMBERS, :]
    means = jnp.sum(state, axis=0, keepdims=True) * (1.0 / MEMBERS)
    anomalies = state - means
    eye = (
        lax.broadcasted_iota(jnp.int32, (MEMBERS, 128), 0)
        == lax.broadcasted_iota(jnp.int32, (MEMBERS, 128), 1)
    ).astype(F32)

    def batch(b, carry):
        anomalies, means, turn = carry
        base = order_ref[b] * BATCH
        for j in range(BATCH):
            k = base + j
            r = var_ref[k]
            val = value_ref[k]
            own = own_ref[pl.ds(k, 1), :]
            row = mask_ref[pl.ds(k, 1), :]
            a = jnp.broadcast_to(anomalies[:, j : j + 1], (MEMBERS, 128))
            m = jnp.broadcast_to(means[:, j : j + 1], (1, 128))
            v = jnp.sum(a * a, axis=0, keepdims=True) * (1.0 / (MEMBERS - 1)) + EPSILON
            cov = jnp.sum(anomalies * a, axis=0, keepdims=True) * row
            cov_own = jnp.sum(turn * a, axis=0, keepdims=True) * own
            whole = v + r
            shrink = 1.0 / (whole + jnp.sqrt(r * whole))
            shift = (val - m) / whole
            anomalies = anomalies - (cov * shrink) * a
            means = means + cov * shift
            turn = turn + cov_own * (shift - shrink * a)
        mask_ref[...] = pltpu.roll(mask_ref[...], 128 - BATCH, 1)
        return (
            pltpu.roll(anomalies, 128 - BATCH, 1),
            pltpu.roll(means, 128 - BATCH, 1),
            turn,
        )

    _, _, turn = lax.fori_loop(0, NOBS // BATCH, batch, (anomalies, means, eye))
    high = turn.astype(BF16).astype(F32)
    low = (turn - high)[:, :MEMBERS]
    high = high[:, :MEMBERS]
    left = jnp.concatenate([high, high, low], axis=1).astype(BF16)

    def plane(p, _):
        for h in range(4):
            cells = slice(256 * h, 256 * h + 256)
            right = jnp.concatenate([f_ref[p, :, cells], f_ref[p, :MEMBERS, cells]], axis=0)
            result = jnp.dot(left, right, preferred_element_type=F32)
            for i in range(2):
                turned[pl.ds(2 * h + i, MEMBERS, stride=8), :] = result[:, 128 * i : 128 * i + 128]
        out_ref[pl.ds(p * MEMBERS, MEMBERS)] = (
            turned[...].reshape(MEMBERS, 8, 128).astype(BF16)
        )
        return 0

    lax.fori_loop(0, PLANES, plane, 0)


def per_device(prior_state, courant, obs_tile, obs_site, obs_value, obs_var, loc_bits, batch_order):
    prior = prior_state.reshape(ROWS, 8, 128)
    wind = courant.reshape(2 * LEVELS, 8, 128)
    me = (lax.axis_index("lat") * N_LON + lax.axis_index("lon")).astype(jnp.int32)[None]
    dma = pltpu.SemaphoreType.DMA
    forecast, observed = pl.pallas_call(
        exchange_kernel,
        out_shape=(
            jax.ShapeDtypeStruct((PLANES, 2 * MEMBERS, CELLS), BF16),
            jax.ShapeDtypeStruct((GROUP, 2, 128), F32),
        ),
        in_specs=[spec(SM)] * 3 + [spec(VM)] * 2,
        out_specs=(spec(VM), spec(VM)),
        scratch_shapes=[
            VM((MEMBERS * 8, 128), F32),
            VM((PLANES, 10, MEMBERS, 128), BF16),
            VM((2, MEMBERS, 128), BF16),
            VM((2, MEMBERS, 128), BF16),
            VM((GROUP, 2, 128), F32),
            VM((GROUP, 2, 128), F32),
            VM((2, 128), F32),
            VM((N_Z, 2, 128), F32),
            VM((2, 128), F32),
            dma((4,)),
            dma((4,)),
            dma((3,)),
            dma((3,)),
        ],
        compiler_params=pltpu.CompilerParams(collective_id=0, has_side_effects=True),
        name="exchange",
    )(obs_tile, obs_site, batch_order, prior, wind)
    analysis = pl.pallas_call(
        filter_kernel,
        out_shape=jax.ShapeDtypeStruct((ROWS, 8, 128), BF16),
        in_specs=[spec(SM)] * 5 + [spec(VM)] * 3,
        out_specs=spec(VM),
        scratch_shapes=[
            VM((128, 128), F32),
            VM((NOBS, 128), F32),
            VM((NOBS, 128), F32),
            VM((MEMBERS * 8, 128), F32),
        ],
        name="filter",
    )(me, obs_tile, batch_order, obs_value, obs_var, loc_bits, observed, forecast)
    return analysis.reshape(prior_state.shape)


def solution(mesh):
    placed = (
        P(None, None, None, "lat", "lon"),
        P(None, None, "lat", "lon"),
        P(),
        P(),
        P(),
        P(),
        P(),
        P(),
    )
    return jax.shard_map(
        per_device,
        mesh=mesh,
        in_specs=placed,
        out_specs=P(None, None, None, "lat", "lon"),
        check_vma=False,
    )
```

time: 78.5 us -> 62.3 us (0.79)
  Pallas kernels: 76.7 us -> 60.6 us
    pallas_call x4 -> x1, Pallas kernels: 62.4 us -> 46.4 us  [per_device(): pl.pallas_call(exchange_kernel, out_shape=(jax.ShapeDtypeStruct((PLANES,...]
where the time goes in v2:
time: 62.3 us; the launch traced here: 62 us
  Pallas kernels  60.6 us (97%)
  local copies, waits for them, and re-layouts  1.4 us (2%)
    pallas_call x1, Pallas kernels, per_device(): pl.pallas_call(exchange_kernel, out_shape=(jax.ShapeDtypeStruct((PLANES,...  46.4 us
    pallas_call x1, Pallas kernels, per_device(): pl.pallas_call(filter_kernel, out_shape=jax.ShapeDtypeStruct((ROWS, 8, 12...  14.2 us
    unnamed x1, local copies, waits for them, and re-layouts  1.4 us

profile of v2, /device:TPU:1, one launch (start us, length us, event | category | flops | bytes accessed | tf_op | source)
XLA Modules:
  0.0 62.0 jit_solution(14086702075481712713)
XLA Ops:
  0.0 1.4 %copy.9.bits_ref = s32[64,18]{1,0:T(8,128)} copy(s32[64,18]{0,1:T(8,128)} %param.14) | data formatting | bytes 9216 | tf_op args[6]
  1.4 46.4 %exchange.1 = (bf16[8,160,1024]{2,1,0:T(8,128)(2,1)}, f32[32,2,128]{2,1,0:T(2,128)}) custom-call(s32[64]{0:T(128)} %tile_ref.3, s32[64]{0:T(128)} %site_ref.1, s32[4]{0:T(128)} %order_ref.3, bf16[640,8,128]{2,1,0:T(8,128)(2,1)} %bitcast.4, f32[8,8,128]{2,1,0:T(8,128)} %bitcast.5), custom_call_target="tpu_custom_call" | custom-call | tf_op jit(solution)/shard_map/exchange/pallas_call | solution.py:423
  47.9 14.2 %filter.1 = bf16[640,8,128]{2,1,0:T(8,128)(2,1)} custom-call(s32[1]{0:T(128)} %bitcast.me_ref, s32[64]{0:T(128)} %tile_ref.3, s32[4]{0:T(128)} %order_ref.3, f32[64]{0:T(128)} %value_ref.1, f32[64]{0:T(128)} %var_ref.1, s32[64,18]{1,0:T(8,128)} %copy.9.bits_ref, f32[32,2,128]{2,1,0:T(2,128)} %get-tuple-element.7.obs_ref, ...), custom_call_target="tpu_custom_call" | custom-call | tf_op jit(solution)/shard_map/filter/pallas_call | solution.py:449

commit v3 on v2

--- a/solution.py
+++ b/solution.py
@@ -32,10 +32,14 @@
     tile_ref,
     site_ref,
     order_ref,
+    prior_hbm,
+    wind_ref,
+    bits_ref,
+    f_hbm,
+    out_ref,
+    mask_ref,
     prior_ref,
-    wind_ref,
     f_ref,
-    out_ref,
     wide,
     rows,
     edge_cols,
@@ -49,6 +53,8 @@
     halo_recv,
     send,
     recv,
+    load_sem,
+    store_sem,
 ):
     lat = lax.axis_index("lat")
     lon = lax.axis_index("lon")
@@ -78,6 +84,8 @@
     def loop(first, count, body):
         lax.fori_loop(first, count, lambda d, c: (body(d), c)[1], 0)
 
+    load = pltpu.make_async_copy(prior_hbm, prior_ref, load_sem)
+    load.start()
     barrier = pltpu.get_barrier_semaphore()
 
     def greet(peer):
@@ -87,6 +95,7 @@
     loop(1, GROUP, lambda d: greet(group_id(other(d))))
     greet(east)
     greet(west)
+    load.wait()
 
     lanes = lax.broadcasted_iota(jnp.int32, (MEMBERS, 128), 1)
 
@@ -154,7 +163,7 @@
     fill = jnp.zeros((128 - MEMBERS, 128), BF16)
     place = lax.broadcasted_iota(jnp.int32, (NOBS, 128), 0)
 
-    def slot(n, carry):
+    def slot(carry):
         lo, hi, table = carry
         use_hi = lo == 0
         word = jnp.where(use_hi, hi, lo)
@@ -210,8 +219,13 @@
         table = jnp.where(place == spot, f, table)
         return lo_next, hi_next, table
 
+    def slots(n, carry):
+        for _ in range(4):
+            carry = slot(carry)
+        return carry
+
     _, _, table = lax.fori_loop(
-        0, BATCH, slot, (halves[0], halves[1], jnp.zeros((NOBS, 128), F32))
+        0, BATCH // 4, slots, (halves[0], halves[1], jnp.zeros((NOBS, 128), F32))
     )
     for n in range(GROUP):
         mine_obs[n] = table[2 * n : 2 * n + 2, :]
@@ -257,6 +271,9 @@
         )
 
     lane16 = lax.broadcasted_iota(jnp.int32, (16, 128), 1)
+
+    def store(p):
+        return pltpu.make_async_copy(f_ref.at[p], f_hbm.at[p], store_sem.at[p])
 
     def forecast(p):
         level = lax.rem(p, LEVELS)
@@ -293,6 +310,28 @@
                 f_ref[p, some, cells] = big
                 low = slice(MEMBERS + 16 * g, MEMBERS + 16 * g + 16)
                 f_ref[p, low, cells] = (f - big.astype(F32)).astype(BF16)
+        store(p).start()
+
+    def masks():
+        owner = jnp.zeros((NOBS, 128), jnp.int32)
+        for q in range(NOBS):
+            k = order_ref[q // BATCH] * BATCH + q % BATCH
+            owner = jnp.where(place == q, tile_ref[k], owner)
+        word_of = owner // 30
+        bit_of = owner - word_of * 30
+        own_word = me // 30
+        own_bit = jnp.full((8, NOBS), lax.rem(me, 30), jnp.int32)
+        chosen = jnp.zeros((NOBS, NOBS), jnp.int32)
+        own = jnp.zeros((8, NOBS), jnp.int32)
+        for w in range(18):
+            word = bits_ref[w : w + 1, :]
+            chosen = jnp.where(word_of[:, :NOBS] == w, word, chosen)
+            own = jnp.where(jnp.full((8, NOBS), own_word, jnp.int32) == w, word, own)
+        scale = 1.0 / (MEMBERS - 1)
+        hit = jnp.bitwise_and(jnp.right_shift(chosen, bit_of[:, :NOBS]), 1)
+        own_hit = jnp.bitwise_and(jnp.right_shift(own, own_bit), 1)
+        mask_ref[:NOBS, :] = hit.astype(F32) * scale
+        mask_ref[NOBS:, :] = own_hit.astype(F32) * scale
 
     loop(1, GROUP, lambda d: copy1(other(d), d).start())
     loop(0, 2, forecast)
@@ -302,6 +341,7 @@
         acc = acc + got1[d]
     part[...] = acc
     loop(0, N_Z - 1, lambda n: copy2(z_step(n)).start())
+    masks()
     loop(2, 6, forecast)
     bulk(got2, N_Z - 1, 1).wait_recv()
     acc = part[...]
@@ -314,52 +354,41 @@
     bulk(out_ref, GROUP - 1, 2).wait_recv()
     for copy in halos:
         copy.wait_send()
+    for p in range(PLANES):
+        store(p).wait()
     bulk(got1, GROUP - 1, 0).wait_send()
     bulk(got2, N_Z - 1, 1).wait_send()
     bulk(got1, GROUP - 1, 2).wait_send()
 
 
 def filter_kernel(
-    me_ref,
-    tile_ref,
     order_ref,
     value_ref,
     var_ref,
     bits_ref,
     obs_ref,
-    f_ref,
-    out_ref,
+    f_hbm,
+    out_hbm,
     table,
     mask_ref,
     own_ref,
     turned,
+    f_ref,
+    out_ref,
+    load_sem,
+    store_sem,
 ):
-    me = me_ref[0]
+    load = pltpu.make_async_copy(f_hbm, f_ref, load_sem)
+    load.start()
     for n in range(GROUP):
         table[2 * n : 2 * n + 2, :] = obs_ref[n]
     table[NOBS:, :] = jnp.zeros((128 - NOBS, 128), F32)
-    lane = lax.broadcasted_iota(jnp.int32, (1, 128), 1)
-
-    def put(q, row):
-        k = order_ref[q // BATCH] * BATCH + lax.rem(q, BATCH)
-        return jnp.where(lane == q, tile_ref[k], row)
-
-    owners = lax.fori_loop(0, NOBS, put, jnp.zeros((1, 128), jnp.int32))
-    word_of = owners // 30
-    bit_of = owners - word_of * 30
-    own_word = me // 30
-    words = bits_ref[...]
-    chosen = jnp.zeros((NOBS, 128), jnp.int32)
-    chosen_own = jnp.zeros((NOBS, 128), jnp.int32)
-    for w in range(18):
-        word = jnp.broadcast_to(words[:, w : w + 1], (NOBS, 128))
-        chosen = jnp.where(word_of == w, word, chosen)
-        chosen_own = jnp.where(own_word == w, word, chosen_own)
-    scale = 1.0 / (MEMBERS - 1)
-    mask_ref[...] = jnp.bitwise_and(jnp.right_shift(chosen, bit_of), 1).astype(F32) * scale
-    own_bit = jnp.full((NOBS, 128), lax.rem(me, 30), jnp.int32)
-    own_ref[...] = jnp.bitwise_and(jnp.right_shift(chosen_own, own_bit), 1).astype(F32) * scale
     state = jnp.transpose(table[...])[:MEMBERS, :]
+    table[...] = jnp.zeros((128, 128), F32)
+    table[: NOBS + 8, :NOBS] = bits_ref[...]
+    masks = jnp.transpose(table[...])[:NOBS, :]
+    mask_ref[...] = masks
+    own_ref[...] = jnp.broadcast_to(masks[:, NOBS : NOBS + 1], (NOBS, 128))
     means = jnp.sum(state, axis=0, keepdims=True) * (1.0 / MEMBERS)
     anomalies = state - means
     eye = (
@@ -367,26 +396,38 @@
         == lax.broadcasted_iota(jnp.int32, (MEMBERS, 128), 1)
     ).astype(F32)
 
+    def spread(x, j):
+        return jnp.broadcast_to(x[:, j : j + 1], (x.shape[0], 128))
+
+    def total(x):
+        return jnp.sum(x, axis=0, keepdims=True)
+
     def batch(b, carry):
         anomalies, means, turn = carry
         base = order_ref[b] * BATCH
+        a = spread(anomalies, 0)
+        m = spread(means, 0)
         for j in range(BATCH):
             k = base + j
             r = var_ref[k]
             val = value_ref[k]
             own = own_ref[pl.ds(k, 1), :]
             row = mask_ref[pl.ds(k, 1), :]
-            a = jnp.broadcast_to(anomalies[:, j : j + 1], (MEMBERS, 128))
-            m = jnp.broadcast_to(means[:, j : j + 1], (1, 128))
-            v = jnp.sum(a * a, axis=0, keepdims=True) * (1.0 / (MEMBERS - 1)) + EPSILON
-            cov = jnp.sum(anomalies * a, axis=0, keepdims=True) * row
-            cov_own = jnp.sum(turn * a, axis=0, keepdims=True) * own
-            whole = v + r
+            whole = total(a * a) * (1.0 / (MEMBERS - 1)) + (r + EPSILON)
             shrink = 1.0 / (whole + jnp.sqrt(r * whole))
             shift = (val - m) / whole
+            if j + 1 < BATCH:
+                after = spread(anomalies, j + 1)
+                link = total(after * a) * spread(row, j + 1)
+                a_next = after - (link * shrink) * a
+                m_next = spread(means, j + 1) + link * shift
+            cov = total(anomalies * a) * row
+            cov_own = total(turn * a) * own
             anomalies = anomalies - (cov * shrink) * a
             means = means + cov * shift
             turn = turn + cov_own * (shift - shrink * a)
+            if j + 1 < BATCH:
+                a, m = a_next, m_next
         mask_ref[...] = pltpu.roll(mask_ref[...], 128 - BATCH, 1)
         return (
             pltpu.roll(anomalies, 128 - BATCH, 1),
@@ -399,6 +440,11 @@
     low = (turn - high)[:, :MEMBERS]
     high = high[:, :MEMBERS]
     left = jnp.concatenate([high, high, low], axis=1).astype(BF16)
+    load.wait()
+
+    def store(p):
+        block = pl.ds(p * MEMBERS, MEMBERS)
+        return pltpu.make_async_copy(out_ref.at[block], out_hbm.at[block], store_sem.at[p])
 
     def plane(p, _):
         for h in range(4):
@@ -410,25 +456,30 @@
         out_ref[pl.ds(p * MEMBERS, MEMBERS)] = (
             turned[...].reshape(MEMBERS, 8, 128).astype(BF16)
         )
+        store(p).start()
         return 0
 
     lax.fori_loop(0, PLANES, plane, 0)
+    for p in range(PLANES):
+        store(p).wait()
 
 
 def per_device(prior_state, courant, obs_tile, obs_site, obs_value, obs_var, loc_bits, batch_order):
     prior = prior_state.reshape(ROWS, 8, 128)
     wind = courant.reshape(2 * LEVELS, 8, 128)
-    me = (lax.axis_index("lat") * N_LON + lax.axis_index("lon")).astype(jnp.int32)[None]
     dma = pltpu.SemaphoreType.DMA
-    forecast, observed = pl.pallas_call(
+    forecast, observed, masks = pl.pallas_call(
         exchange_kernel,
         out_shape=(
             jax.ShapeDtypeStruct((PLANES, 2 * MEMBERS, CELLS), BF16),
             jax.ShapeDtypeStruct((GROUP, 2, 128), F32),
+            jax.ShapeDtypeStruct((NOBS + 8, NOBS), F32),
         ),
-        in_specs=[spec(SM)] * 3 + [spec(VM)] * 2,
-        out_specs=(spec(VM), spec(VM)),
+        in_specs=[spec(SM)] * 3 + [spec(pl.ANY)] + [spec(VM)] * 2,
+        out_specs=(spec(pl.ANY), spec(VM), spec(VM)),
         scratch_shapes=[
+            VM((ROWS, 8, 128), BF16),
+            VM((PLANES, 2 * MEMBERS, CELLS), BF16),
             VM((MEMBERS * 8, 128), F32),
             VM((PLANES, 10, MEMBERS, 128), BF16),
             VM((2, MEMBERS, 128), BF16),
@@ -442,23 +493,29 @@
             dma((4,)),
             dma((3,)),
             dma((3,)),
+            dma,
+            dma((PLANES,)),
         ],
         compiler_params=pltpu.CompilerParams(collective_id=0, has_side_effects=True),
         name="exchange",
-    )(obs_tile, obs_site, batch_order, prior, wind)
+    )(obs_tile, obs_site, batch_order, prior, wind, loc_bits.T)
     analysis = pl.pallas_call(
         filter_kernel,
         out_shape=jax.ShapeDtypeStruct((ROWS, 8, 128), BF16),
-        in_specs=[spec(SM)] * 5 + [spec(VM)] * 3,
-        out_specs=spec(VM),
+        in_specs=[spec(SM)] * 3 + [spec(VM)] * 2 + [spec(pl.ANY)],
+        out_specs=spec(pl.ANY),
         scratch_shapes=[
             VM((128, 128), F32),
             VM((NOBS, 128), F32),
             VM((NOBS, 128), F32),
             VM((MEMBERS * 8, 128), F32),
+            VM((PLANES, 2 * MEMBERS, CELLS), BF16),
+            VM((ROWS, 8, 128), BF16),
+            dma,
+            dma((PLANES,)),
         ],
         name="filter",
-    )(me, obs_tile, batch_order, obs_value, obs_var, loc_bits, observed, forecast)
+    )(batch_order, obs_value, obs_var, masks, observed, forecast)
     return analysis.reshape(prior_state.shape)
 
 

time: 62.3 us -> 52.5 us (0.84)
  Pallas kernels: 60.6 us -> 52.2 us
  local copies, waits for them, and re-layouts: 1.4 us -> 0 us
    pallas_call x1, Pallas kernels: 14.2 us -> 8.92 us  [per_device(): pl.pallas_call(filter_kernel, out_shape=jax.ShapeDtypeStruct((ROWS, 8, 12...]
    pallas_call x1, Pallas kernels: 46.4 us -> 43.3 us  [per_device(): pl.pallas_call(exchange_kernel, out_shape=(jax.ShapeDtypeStruct((PLANES,...]
    unnamed x1 -> x0, local copies, waits for them, and re-layouts: 1.4 us -> none
where the time goes in v3:
time: 52.5 us; the launch traced here: 52.2 us
  Pallas kernels  52.2 us (99%)
    pallas_call x1, Pallas kernels, per_device(): pl.pallas_call(exchange_kernel, out_shape=(jax.ShapeDtypeStruct((PLANES,...  43.3 us
    pallas_call x1, Pallas kernels, per_device(): pl.pallas_call(filter_kernel, out_shape=jax.ShapeDtypeStruct((ROWS, 8, 12...  8.92 us

profile of v3, /device:TPU:1, one launch (start us, length us, event | category | flops | bytes accessed | tf_op | source)
XLA Modules:
  0.0 52.2 jit_solution(5311564157928385300)
XLA Ops:
  0.0 43.3 %exchange.1 = (bf16[8,160,1024]{2,1,0:T(8,128)(2,1)}, f32[32,2,128]{2,1,0:T(2,128)}, f32[72,64]{1,0:T(8,128)}) custom-call(s32[64]{0:T(128)} %tile_ref.1, s32[64]{0:T(128)} %site_ref.1, s32[4]{0:T(128)} %order_ref.3, bf16[640,8,128]{2,1,0:T(8,128)(2,1)} %bitcast.4, f32[8,8,128]{2,1,0:T(8,128)} %bitcast.5, s32[18,64]{1,0:T(8,128)} %bitcast.6), custom_call_target="tpu_custom_call" | custom-call | tf_op jit(solution)/shard_map/exchange/pallas_call | solution.py:471
  43.3 8.9 %filter.1 = bf16[640,8,128]{2,1,0:T(8,128)(2,1)} custom-call(s32[4]{0:T(128)} %order_ref.3, f32[64]{0:T(128)} %value_ref.1, f32[64]{0:T(128)} %var_ref.1, f32[72,64]{1,0:T(8,128)} %get-tuple-element.8.bits_ref, f32[32,2,128]{2,1,0:T(2,128)} %get-tuple-element.9.obs_ref, bf16[8,160,1024]{2,1,0:T(8,128)(2,1)} %get-tuple-element.10.f_hbm), custom_call_target="tpu_custom_call" | custom-call | tf_op jit(solution)/shard_map/filter/pallas_call | solution.py:502

commit v4 on v3

--- a/solution.py
+++ b/solution.py
@@ -44,6 +44,9 @@
     rows,
     edge_cols,
     halo_cols,
+    halo_rows,
+    near,
+    halo_near,
     mine_obs,
     got1,
     part,
@@ -55,6 +58,8 @@
     recv,
     load_sem,
     store_sem,
+    row_send,
+    row_recv,
 ):
     lat = lax.axis_index("lat")
     lon = lax.axis_index("lon")
@@ -106,12 +111,12 @@
                 wide[pl.ds(at, 8), :] = prior_ref[p * MEMBERS + g * 16 + i].astype(F32)
             for r in range(8):
                 part_rows = wide[pl.ds(g * 128 + r, 16, stride=8), :]
-                rows[p, r + 1, pl.ds(pl.multiple_of(g * 16, 16), 16), :] = part_rows.astype(BF16)
+                rows[p, r, pl.ds(pl.multiple_of(g * 16, 16), 16), :] = part_rows.astype(BF16)
 
         loop(0, 5, block)
         first, last = acc
         for r in range(8):
-            x = rows[p, r + 1].astype(F32)
+            x = rows[p, r].astype(F32)
             here = lanes == p * 8 + r
             first = jnp.where(here, pltpu.roll(x, p * 8 + r, 1), first)
             last = jnp.where(here, pltpu.roll(x, p * 8 + r + 1, 1), last)
@@ -132,12 +137,37 @@
             owned = owned | (hit << n)
         halves.append(owned)
 
+    place = lax.broadcasted_iota(jnp.int32, (NOBS, 128), 0)
+    wide_lane = lax.broadcasted_iota(jnp.int32, (NOBS, 128), 1)
+    owner = jnp.zeros((NOBS, 128), jnp.int32)
+    site = jnp.zeros((NOBS, 128), jnp.int32)
+    for q in range(NOBS):
+        k = order_ref[q // BATCH] * BATCH + q % BATCH
+        owner = jnp.where(place == q, tile_ref[k], owner)
+        site = jnp.where(place == q, site_ref[k], site)
+    fill = jnp.zeros((128 - MEMBERS, 128), BF16)
+
+    def pick_edge(tile, wanted, r):
+        code = jnp.where(owner == tile, site - wanted * 128, -1)
+        found = jnp.zeros((NOBS, 128), F32)
+        for p in range(PLANES):
+            found = found + lax.dot_general(
+                (code == wide_lane + p * CELLS).astype(BF16),
+                jnp.concatenate([rows[p, r], fill], axis=0),
+                (((1,), (1,)), ((), ())),
+                preferred_element_type=F32,
+            )
+        return found.astype(BF16)
+
+    near[0] = pick_edge(me + N_LON, 0, 7)
+    near[1] = pick_edge(me - N_LON, 7, 0)
+
     pl.semaphore_wait(barrier, GROUP - 1 + N_Z - 1 + 2)
     halos = []
     for n, (src, dst, peer) in enumerate(
         (
-            (rows.at[:, 8], rows.at[:, 0], north),
-            (rows.at[:, 1], rows.at[:, 9], south),
+            (near.at[0], halo_near.at[0], north),
+            (near.at[1], halo_near.at[1], south),
             (edge_cols.at[0], halo_cols.at[0], east),
             (edge_cols.at[1], halo_cols.at[1], west),
         )
@@ -152,19 +182,13 @@
         )
         copy.start()
         halos.append(copy)
-    for copy in halos:
-        copy.wait_recv()
-
     has_south = (lat > 0).astype(F32)
     has_north = (lat < N_LAT - 1).astype(F32)
-    for p in range(PLANES):
-        rows[p, 0] = (rows[p, 0].astype(F32) * has_south).astype(BF16)
-        rows[p, 9] = (rows[p, 9].astype(F32) * has_north).astype(BF16)
-    fill = jnp.zeros((128 - MEMBERS, 128), BF16)
-    place = lax.broadcasted_iota(jnp.int32, (NOBS, 128), 0)
+
+    lane1 = lax.broadcasted_iota(jnp.int32, (1, 128), 1)
 
     def slot(carry):
-        lo, hi, table = carry
+        lo, hi, table, factors = carry
         use_hi = lo == 0
         word = jnp.where(use_hi, hi, lo)
         low = word & (-word)
@@ -183,19 +207,20 @@
         r = (s // 128) % 8
         c = s % 128
         around = jnp.concatenate(
-            [rows[p, r + 1], fill, rows[p, r], fill, rows[p, r + 2], fill], axis=0
+            [
+                rows[p, r],
+                fill,
+                rows[p, jnp.maximum(r - 1, 0)],
+                fill,
+                rows[p, jnp.minimum(r + 1, 7)],
+                fill,
+            ],
+            axis=0,
         )
         shift = jnp.where(sub == 1, -1, jnp.where(sub == 2, 1, 0))
         pick = (lane == c + shift).astype(BF16)
         found = lax.dot_general(
             pick, around, (((1,), (1,)), ((), ())), preferred_element_type=F32
-        )
-        sides = jnp.concatenate([halo_cols[0], fill, halo_cols[1], fill], axis=0)
-        beside = lax.dot_general(
-            (lane == p * 8 + r).astype(BF16),
-            sides,
-            (((1,), (1,)), ((), ())),
-            preferred_element_type=F32,
         )
         at_cell = (sub == r) & (lane == c)
         level = p % LEVELS
@@ -204,28 +229,54 @@
         cu = jnp.sum(cu, axis=1, keepdims=True)
         cv = jnp.sum(cv, axis=1, keepdims=True)
         x = found[0:1, 0:128]
-        column = jnp.full((1, 128), c, jnp.int32)
-        xw = jnp.where(column == 0, beside[0:1, 0:128], found[1:2, 0:128])
-        xe = jnp.where(column == 127, beside[0:1, 128:256], found[2:3, 0:128])
-        xs = found[0:1, 128:256]
-        xn = found[0:1, 256:384]
+        xw = found[1:2, 0:128]
+        xe = found[2:3, 0:128]
+        xs = found[0:1, 128:256] * (r > 0).astype(F32)
+        xn = found[0:1, 256:384] * (r < 7).astype(F32)
+        cu_up, cu_dn = jnp.maximum(cu, 0.0), jnp.minimum(cu, 0.0)
+        cv_up, cv_dn = jnp.maximum(cv, 0.0), jnp.minimum(cv, 0.0)
         f = (
             x
-            - jnp.maximum(cu, 0.0) * (x - xw)
-            - jnp.minimum(cu, 0.0) * (xe - x)
-            - jnp.maximum(cv, 0.0) * (x - xs)
-            - jnp.minimum(cv, 0.0) * (xn - x)
-        )
+            - cu_up * (x - xw)
+            - cu_dn * (xe - x)
+            - cv_up * (x - xs)
+            - cv_dn * (xn - x)
+        )
+        four = (
+            jnp.where(lane1 == 0, cu_up * (c == 0).astype(F32), 0.0)
+            - jnp.where(lane1 == 1, cu_dn * (c == 127).astype(F32), 0.0)
+            + jnp.where(lane1 == 2, cv_up * (r == 0).astype(F32), 0.0)
+            - jnp.where(lane1 == 3, cv_dn * (r == 7).astype(F32), 0.0)
+        )
+        factors = jnp.where(place == spot, four, factors)
         table = jnp.where(place == spot, f, table)
-        return lo_next, hi_next, table
+        return lo_next, hi_next, table, factors
 
     def slots(n, carry):
         for _ in range(4):
             carry = slot(carry)
         return carry
 
-    _, _, table = lax.fori_loop(
-        0, BATCH // 4, slots, (halves[0], halves[1], jnp.zeros((NOBS, 128), F32))
+    blank = jnp.zeros((NOBS, 128), F32)
+    _, _, table, factors = lax.fori_loop(
+        0, BATCH // 4, slots, (halves[0], halves[1], blank, blank)
+    )
+    for copy in halos:
+        copy.wait_recv()
+    row_of = jnp.bitwise_and(jnp.right_shift(site, 7), 7)
+    plane_of = jnp.right_shift(site, 10)
+    beside = lax.dot_general(
+        (wide_lane == plane_of * 8 + row_of).astype(BF16),
+        jnp.concatenate([halo_cols[0], fill, halo_cols[1], fill], axis=0),
+        (((1,), (1,)), ((), ())),
+        preferred_element_type=F32,
+    )
+    table = (
+        table
+        + factors[:, 0:1] * beside[:, 0:128]
+        + factors[:, 1:2] * beside[:, 128:256]
+        + factors[:, 2:3] * halo_near[0].astype(F32)
+        + factors[:, 3:4] * halo_near[1].astype(F32)
     )
     for n in range(GROUP):
         mine_obs[n] = table[2 * n : 2 * n + 2, :]
@@ -286,9 +337,15 @@
             cells = slice(128 * r, 128 * r + 128)
             for g in range(5):
                 some = slice(16 * g, 16 * g + 16)
-                x = rows[p, r + 1, some, :].astype(F32)
-                xs = rows[p, r, some, :].astype(F32)
-                xn = rows[p, r + 2, some, :].astype(F32)
+                x = rows[p, r, some, :].astype(F32)
+                if r > 0:
+                    xs = rows[p, r - 1, some, :].astype(F32)
+                else:
+                    xs = halo_rows[0, p, some, :].astype(F32) * has_south
+                if r < 7:
+                    xn = rows[p, r + 1, some, :].astype(F32)
+                else:
+                    xn = halo_rows[1, p, some, :].astype(F32) * has_north
                 from_west = halo_cols[0, some, :].astype(F32)
                 from_east = halo_cols[1, some, :].astype(F32)
                 xw = jnp.where(
@@ -313,10 +370,6 @@
         store(p).start()
 
     def masks():
-        owner = jnp.zeros((NOBS, 128), jnp.int32)
-        for q in range(NOBS):
-            k = order_ref[q // BATCH] * BATCH + q % BATCH
-            owner = jnp.where(place == q, tile_ref[k], owner)
         word_of = owner // 30
         bit_of = owner - word_of * 30
         own_word = me // 30
@@ -334,15 +387,25 @@
         mask_ref[NOBS:, :] = own_hit.astype(F32) * scale
 
     loop(1, GROUP, lambda d: copy1(other(d), d).start())
-    loop(0, 2, forecast)
+    masks()
     bulk(got1, GROUP - 1, 0).wait_recv()
     acc = mine_obs[mine]
     for d in range(1, GROUP):
         acc = acc + got1[d]
     part[...] = acc
     loop(0, N_Z - 1, lambda n: copy2(z_step(n)).start())
-    masks()
-    loop(2, 6, forecast)
+    strips = []
+    for n, (src, peer) in enumerate(((rows.at[:, 7], north), (rows.at[:, 0], south))):
+        copy = pltpu.make_async_remote_copy(
+            src_ref=src,
+            dst_ref=halo_rows.at[n],
+            send_sem=row_send.at[n],
+            recv_sem=row_recv.at[n],
+            device_id=peer,
+            device_id_type=MESH,
+        )
+        copy.start()
+        strips.append(copy)
     bulk(got2, N_Z - 1, 1).wait_recv()
     acc = part[...]
     for d in range(1, N_Z):
@@ -350,9 +413,11 @@
     total[...] = acc
     loop(1, GROUP, lambda d: copy3(other(d)).start())
     out_ref[mine] = acc
-    loop(6, PLANES, forecast)
+    for copy in strips:
+        copy.wait_recv()
+    loop(0, PLANES, forecast)
     bulk(out_ref, GROUP - 1, 2).wait_recv()
-    for copy in halos:
+    for copy in halos + strips:
         copy.wait_send()
     for p in range(PLANES):
         store(p).wait()
@@ -481,9 +546,12 @@
             VM((ROWS, 8, 128), BF16),
             VM((PLANES, 2 * MEMBERS, CELLS), BF16),
             VM((MEMBERS * 8, 128), F32),
-            VM((PLANES, 10, MEMBERS, 128), BF16),
+            VM((PLANES, 8, MEMBERS, 128), BF16),
             VM((2, MEMBERS, 128), BF16),
             VM((2, MEMBERS, 128), BF16),
+            VM((2, PLANES, MEMBERS, 128), BF16),
+            VM((2, NOBS, 128), BF16),
+            VM((2, NOBS, 128), BF16),
             VM((GROUP, 2, 128), F32),
             VM((GROUP, 2, 128), F32),
             VM((2, 128), F32),
@@ -495,6 +563,8 @@
             dma((3,)),
             dma,
             dma((PLANES,)),
+            dma((2,)),
+            dma((2,)),
         ],
         compiler_params=pltpu.CompilerParams(collective_id=0, has_side_effects=True),
         name="exchange",

time: 52.5 us -> 48.8 us (0.930)
  Pallas kernels: 52.2 us -> 48.5 us
    pallas_call x1, Pallas kernels: 43.3 us -> 39.6 us  [per_device(): pl.pallas_call(exchange_kernel, out_shape=(jax.ShapeDtypeStruct((PLANES,...]
where the time goes in v4:
time: 48.8 us; the launch traced here: 48.5 us
  Pallas kernels  48.5 us (99%)
    pallas_call x1, Pallas kernels, per_device(): pl.pallas_call(exchange_kernel, out_shape=(jax.ShapeDtypeStruct((PLANES,...  39.6 us
    pallas_call x1, Pallas kernels, per_device(): pl.pallas_call(filter_kernel, out_shape=jax.ShapeDtypeStruct((ROWS, 8, 12...  8.92 us

profile of v4, /device:TPU:1, one launch (start us, length us, event | category | flops | bytes accessed | tf_op | source)
XLA Modules:
  0.0 48.5 jit_solution(16517132315317817568)
XLA Ops:
  0.0 39.6 %exchange.1 = (bf16[8,160,1024]{2,1,0:T(8,128)(2,1)}, f32[32,2,128]{2,1,0:T(2,128)}, f32[72,64]{1,0:T(8,128)}) custom-call(s32[64]{0:T(128)} %tile_ref.1, s32[64]{0:T(128)} %site_ref.1, s32[4]{0:T(128)} %order_ref.3, bf16[640,8,128]{2,1,0:T(8,128)(2,1)} %bitcast.4, f32[8,8,128]{2,1,0:T(8,128)} %bitcast.5, s32[18,64]{1,0:T(8,128)} %bitcast.6), custom_call_target="tpu_custom_call" | custom-call | tf_op jit(solution)/shard_map/exchange/pallas_call | solution.py:536
  39.6 8.9 %filter.1 = bf16[640,8,128]{2,1,0:T(8,128)(2,1)} custom-call(s32[4]{0:T(128)} %order_ref.3, f32[64]{0:T(128)} %value_ref.1, f32[64]{0:T(128)} %var_ref.1, f32[72,64]{1,0:T(8,128)} %get-tuple-element.8.bits_ref, f32[32,2,128]{2,1,0:T(2,128)} %get-tuple-element.9.obs_ref, bf16[8,160,1024]{2,1,0:T(8,128)(2,1)} %get-tuple-element.10.f_hbm), custom_call_target="tpu_custom_call" | custom-call | tf_op jit(solution)/shard_map/filter/pallas_call | solution.py:572

commit v5 on v4

--- a/solution.py
+++ b/solution.py
@@ -60,6 +60,8 @@
     store_sem,
     row_send,
     row_recv,
+    ready_up,
+    ready_down,
 ):
     lat = lax.axis_index("lat")
     lon = lax.axis_index("lon")
@@ -96,7 +98,8 @@
     def greet(peer):
         pl.semaphore_signal(barrier, inc=1, device_id=peer, device_id_type=MESH)
 
-    loop(0, N_Z - 1, lambda n: greet(z_id(z_step(n))))
+    greet(z_id(1))
+    greet(z_id(N_Z - 1))
     loop(1, GROUP, lambda d: greet(group_id(other(d))))
     greet(east)
     greet(west)
@@ -162,7 +165,21 @@
     near[0] = pick_edge(me + N_LON, 0, 7)
     near[1] = pick_edge(me - N_LON, 7, 0)
 
-    pl.semaphore_wait(barrier, GROUP - 1 + N_Z - 1 + 2)
+    def tell(step):
+        reach = (1, 2, 4)[step]
+        pl.semaphore_signal(
+            ready_up.at[step], inc=1, device_id=z_id(reach), device_id_type=MESH
+        )
+        pl.semaphore_signal(
+            ready_down.at[step], inc=1, device_id=z_id(N_Z - reach), device_id_type=MESH
+        )
+
+    def hear(step):
+        pl.semaphore_wait(ready_up.at[step], 1)
+        pl.semaphore_wait(ready_down.at[step], 1)
+
+    pl.semaphore_wait(barrier, GROUP - 1 + 2 + 2)
+    tell(0)
     halos = []
     for n, (src, dst, peer) in enumerate(
         (
@@ -258,11 +275,14 @@
         return carry
 
     blank = jnp.zeros((NOBS, 128), F32)
-    _, _, table, factors = lax.fori_loop(
-        0, BATCH // 4, slots, (halves[0], halves[1], blank, blank)
-    )
+    state = lax.fori_loop(0, 2, slots, (halves[0], halves[1], blank, blank))
+    hear(0)
+    tell(1)
+    _, _, table, factors = lax.fori_loop(2, BATCH // 4, slots, state)
     for copy in halos:
         copy.wait_recv()
+    hear(1)
+    tell(2)
     row_of = jnp.bitwise_and(jnp.right_shift(site, 7), 7)
     plane_of = jnp.right_shift(site, 10)
     beside = lax.dot_general(
@@ -388,6 +408,7 @@
 
     loop(1, GROUP, lambda d: copy1(other(d), d).start())
     masks()
+    hear(2)
     bulk(got1, GROUP - 1, 0).wait_recv()
     acc = mine_obs[mine]
     for d in range(1, GROUP):
@@ -565,6 +586,8 @@
             dma((PLANES,)),
             dma((2,)),
             dma((2,)),
+            pltpu.SemaphoreType.REGULAR((3,)),
+            pltpu.SemaphoreType.REGULAR((3,)),
         ],
         compiler_params=pltpu.CompilerParams(collective_id=0, has_side_effects=True),
         name="exchange",

time: 48.8 us -> 48.8 us (level)
  no operation moved by 1% of the time
where the time goes in v5:
time: 48.8 us; the launch traced here: 48.5 us
  Pallas kernels  48.5 us (99%)
    pallas_call x1, Pallas kernels, per_device(): pl.pallas_call(exchange_kernel, out_shape=(jax.ShapeDtypeStruct((PLANES,...  39.6 us
    pallas_call x1, Pallas kernels, per_device(): pl.pallas_call(filter_kernel, out_shape=jax.ShapeDtypeStruct((ROWS, 8, 12...  8.92 us

profile of v5, /device:TPU:1, one launch (start us, length us, event | category | flops | bytes accessed | tf_op | source)
XLA Modules:
  0.0 48.5 jit_solution(18035829331286511958)
XLA Ops:
  0.0 39.6 %exchange.1 = (bf16[8,160,1024]{2,1,0:T(8,128)(2,1)}, f32[32,2,128]{2,1,0:T(2,128)}, f32[72,64]{1,0:T(8,128)}) custom-call(s32[64]{0:T(128)} %tile_ref.1, s32[64]{0:T(128)} %site_ref.1, s32[4]{0:T(128)} %order_ref.3, bf16[640,8,128]{2,1,0:T(8,128)(2,1)} %bitcast.4, f32[8,8,128]{2,1,0:T(8,128)} %bitcast.5, s32[18,64]{1,0:T(8,128)} %bitcast.6), custom_call_target="tpu_custom_call" | custom-call | tf_op jit(solution)/shard_map/exchange/pallas_call | solution.py:557
  39.6 8.9 %filter.1 = bf16[640,8,128]{2,1,0:T(8,128)(2,1)} custom-call(s32[4]{0:T(128)} %order_ref.3, f32[64]{0:T(128)} %value_ref.1, f32[64]{0:T(128)} %var_ref.1, f32[72,64]{1,0:T(8,128)} %get-tuple-element.8.bits_ref, f32[32,2,128]{2,1,0:T(2,128)} %get-tuple-element.9.obs_ref, bf16[8,160,1024]{2,1,0:T(8,128)(2,1)} %get-tuple-element.10.f_hbm), custom_call_target="tpu_custom_call" | custom-call | tf_op jit(solution)/shard_map/filter/pallas_call | solution.py:595

commit v6 on v5

--- a/solution.py
+++ b/solution.py
@@ -85,6 +85,9 @@
     def z_step(n):
         return 8 + ((n + 1) // 2) * (2 * lax.rem(n + 1, 2) - 1)
 
+    def far_step(n):
+        return 16 + ((n + 1) // 2) * (2 * lax.rem(n + 1, 2) - 1)
+
     def z_id(d):
         return (lat, lax.rem(z + d, N_Z) * 2 + core)
 
@@ -346,9 +349,9 @@
     def store(p):
         return pltpu.make_async_copy(f_ref.at[p], f_hbm.at[p], store_sem.at[p])
 
-    def forecast(p):
+    def forecast(p, which):
         level = lax.rem(p, LEVELS)
-        for r in range(8):
+        for r in which:
             cu = wind_ref[level, r : r + 1, :]
             cv = wind_ref[LEVELS + level, r : r + 1, :]
             cu_up, cu_dn = jnp.maximum(cu, 0.0), jnp.minimum(cu, 0.0)
@@ -387,6 +390,12 @@
                 f_ref[p, some, cells] = big
                 low = slice(MEMBERS + 16 * g, MEMBERS + 16 * g + 16)
                 f_ref[p, low, cells] = (f - big.astype(F32)).astype(BF16)
+
+    def inner(p):
+        forecast(p, range(1, 7))
+
+    def outer(p):
+        forecast(p, (0, 7))
         store(p).start()
 
     def masks():
@@ -406,7 +415,7 @@
         mask_ref[:NOBS, :] = hit.astype(F32) * scale
         mask_ref[NOBS:, :] = own_hit.astype(F32) * scale
 
-    loop(1, GROUP, lambda d: copy1(other(d), d).start())
+    loop(0, GROUP - 1, lambda n: copy1(other(far_step(n)), far_step(n)).start())
     masks()
     hear(2)
     bulk(got1, GROUP - 1, 0).wait_recv()
@@ -427,16 +436,17 @@
         )
         copy.start()
         strips.append(copy)
+    loop(0, PLANES, inner)
     bulk(got2, N_Z - 1, 1).wait_recv()
     acc = part[...]
     for d in range(1, N_Z):
         acc = acc + got2[d]
     total[...] = acc
-    loop(1, GROUP, lambda d: copy3(other(d)).start())
+    loop(0, GROUP - 1, lambda n: copy3(other(far_step(n))).start())
     out_ref[mine] = acc
     for copy in strips:
         copy.wait_recv()
-    loop(0, PLANES, forecast)
+    loop(0, PLANES, outer)
     bulk(out_ref, GROUP - 1, 2).wait_recv()
     for copy in halos + strips:
         copy.wait_send()

time: 48.8 us -> 49 us (level)
  no operation moved by 1% of the time
where the time goes in v6:
time: 49 us; the launch traced here: 48.7 us
  Pallas kernels  48.7 us (99%)
    pallas_call x1, Pallas kernels, per_device(): pl.pallas_call(exchange_kernel, out_shape=(jax.ShapeDtypeStruct((PLANES,...  39.8 us
    pallas_call x1, Pallas kernels, per_device(): pl.pallas_call(filter_kernel, out_shape=jax.ShapeDtypeStruct((ROWS, 8, 12...  8.92 us

profile of v6, /device:TPU:1, one launch (start us, length us, event | category | flops | bytes accessed | tf_op | source)
XLA Modules:
  0.0 48.7 jit_solution(12595975366645963005)
XLA Ops:
  0.0 39.8 %exchange.1 = (bf16[8,160,1024]{2,1,0:T(8,128)(2,1)}, f32[32,2,128]{2,1,0:T(2,128)}, f32[72,64]{1,0:T(8,128)}) custom-call(s32[64]{0:T(128)} %tile_ref.1, s32[64]{0:T(128)} %site_ref.1, s32[4]{0:T(128)} %order_ref.3, bf16[640,8,128]{2,1,0:T(8,128)(2,1)} %bitcast.4, f32[8,8,128]{2,1,0:T(8,128)} %bitcast.5, s32[18,64]{1,0:T(8,128)} %bitcast.6), custom_call_target="tpu_custom_call" | custom-call | tf_op jit(solution)/shard_map/exchange/pallas_call | solution.py:567
  39.8 8.9 %filter.1 = bf16[640,8,128]{2,1,0:T(8,128)(2,1)} custom-call(s32[4]{0:T(128)} %order_ref.3, f32[64]{0:T(128)} %value_ref.1, f32[64]{0:T(128)} %var_ref.1, f32[72,64]{1,0:T(8,128)} %get-tuple-element.8.bits_ref, f32[32,2,128]{2,1,0:T(2,128)} %get-tuple-element.9.obs_ref, bf16[8,160,1024]{2,1,0:T(8,128)(2,1)} %get-tuple-element.10.f_hbm), custom_call_target="tpu_custom_call" | custom-call | tf_op jit(solution)/shard_map/filter/pallas_call | solution.py:605

commit v7 on v6

--- a/solution.py
+++ b/solution.py
@@ -85,9 +85,6 @@
     def z_step(n):
         return 8 + ((n + 1) // 2) * (2 * lax.rem(n + 1, 2) - 1)
 
-    def far_step(n):
-        return 16 + ((n + 1) // 2) * (2 * lax.rem(n + 1, 2) - 1)
-
     def z_id(d):
         return (lat, lax.rem(z + d, N_Z) * 2 + core)
 
@@ -415,7 +412,7 @@
         mask_ref[:NOBS, :] = hit.astype(F32) * scale
         mask_ref[NOBS:, :] = own_hit.astype(F32) * scale
 
-    loop(0, GROUP - 1, lambda n: copy1(other(far_step(n)), far_step(n)).start())
+    loop(1, GROUP, lambda d: copy1(other(d), d).start())
     masks()
     hear(2)
     bulk(got1, GROUP - 1, 0).wait_recv()
@@ -442,7 +439,7 @@
     for d in range(1, N_Z):
         acc = acc + got2[d]
     total[...] = acc
-    loop(0, GROUP - 1, lambda n: copy3(other(far_step(n))).start())
+    loop(1, GROUP, lambda d: copy3(other(d)).start())
     out_ref[mine] = acc
     for copy in strips:
         copy.wait_recv()
@@ -496,7 +493,9 @@
         return jnp.broadcast_to(x[:, j : j + 1], (x.shape[0], 128))
 
     def total(x):
-        return jnp.sum(x, axis=0, keepdims=True)
+        half = x[:40] + x[40:]
+        quarter = half[:16] + half[16:32]
+        return jnp.sum(quarter[:8] + quarter[8:] + half[32:], axis=0, keepdims=True)
 
     def batch(b, carry):
         anomalies, means, turn = carry

time: 49 us -> 48.5 us (0.990)
  Pallas kernels: 48.7 us -> 48.2 us
where the time goes in v7:
time: 48.5 us; the launch traced here: 48.2 us
  Pallas kernels  48.2 us (99%)
    pallas_call x1, Pallas kernels, per_device(): pl.pallas_call(exchange_kernel, out_shape=(jax.ShapeDtypeStruct((PLANES,...  39.6 us
    pallas_call x1, Pallas kernels, per_device(): pl.pallas_call(filter_kernel, out_shape=jax.ShapeDtypeStruct((ROWS, 8, 12...  8.62 us

profile of v7, /device:TPU:1, one launch (start us, length us, event | category | flops | bytes accessed | tf_op | source)
XLA Modules:
  0.0 48.2 jit_solution(425526668468035071)
XLA Ops:
  0.0 39.6 %exchange.1 = (bf16[8,160,1024]{2,1,0:T(8,128)(2,1)}, f32[32,2,128]{2,1,0:T(2,128)}, f32[72,64]{1,0:T(8,128)}) custom-call(s32[64]{0:T(128)} %tile_ref.1, s32[64]{0:T(128)} %site_ref.1, s32[4]{0:T(128)} %order_ref.3, bf16[640,8,128]{2,1,0:T(8,128)(2,1)} %bitcast.4, f32[8,8,128]{2,1,0:T(8,128)} %bitcast.5, s32[18,64]{1,0:T(8,128)} %bitcast.6), custom_call_target="tpu_custom_call" | custom-call | tf_op jit(solution)/shard_map/exchange/pallas_call | solution.py:566
  39.6 8.6 %filter.1 = bf16[640,8,128]{2,1,0:T(8,128)(2,1)} custom-call(s32[4]{0:T(128)} %order_ref.3, f32[64]{0:T(128)} %value_ref.1, f32[64]{0:T(128)} %var_ref.1, f32[72,64]{1,0:T(8,128)} %get-tuple-element.8.bits_ref, f32[32,2,128]{2,1,0:T(2,128)} %get-tuple-element.9.obs_ref, bf16[8,160,1024]{2,1,0:T(8,128)(2,1)} %get-tuple-element.10.f_hbm), custom_call_target="tpu_custom_call" | custom-call | tf_op jit(solution)/shard_map/filter/pallas_call | solution.py:604
